TPU v7x, 256 devices: a whole 4x4x8 slice. The times are simulated.
256 devices in a mesh: gx: 8 (over z), gy: 32 (over y, x, core).
Axes of the slice: x: 4, y: 4, z: 8, core: 2. Of those that a mesh axis runs over, the one named last changes fastest.
Arguments:
- velocity: float32 [3, 8, 512, 1024], P(None, 'gx', 'gy'), may hold values from -6 to 6
- y_metric: float32 [512], P('gy'), may hold values from 0.5 to 4
- forward_rate: float32 [3, 512], P(None, 'gy'), may hold values from 0.9921875 to 1
- backward_rate: float32 [3, 512], P(None, 'gy'), may hold values from 0.9921875 to 1
- pivot_inv: float32 [3, 512], P(None, 'gy'), may hold values from 0 to 0.0007324219
- particle_vel: float32 [3, 917504], P(None, ('gx', 'gy')), may hold values from -6 to 6
- particle_cell: int32 [917504], P(('gx', 'gy')), may hold values from 0 to 16383
- particle_offset: float32 [3, 917504], P(None, ('gx', 'gy')), may hold values from 0 to 1
- inverse_tau: float32 [917504], P(('gx', 'gy')), may hold values from 0.5 to 8
- outgoing_count: int32 [8, 32, 3], P('gx', 'gy'), may hold values from 0 to 512, as said below
Outputs:
- velocity_out: float32 [3, 8, 512, 1024], P(None, 'gx', 'gy')
- particle_out: float32 [3, 917504], P(None, ('gx', 'gy'))
Inputs may be any that keep to these rules, and one draw needn't show every extreme that they name: `outgoing_count`: entry d of a block counts the live leading slots of its outgoing block d; the -y block of the lowest and the +y block of the highest wall-normal blocks are empty; some +x block is full.
All inputs are finite; a program needn't handle non-finite values.
Results may differ from a plain program's by a relative error of at most 0.00029.
Values sent between devices are 32-bit elements; how exact they have to be, the bound alone decides.
A program may use at most 192 MiB of HBM per device.

v0:
```python
import jax
import jax.numpy as jnp
from jax import lax
from jax.sharding import PartitionSpec as P

RESIDENT = 2048
CAP = 512
SECTIONS = 3


SECTION_WEIGHTS = (8.0 / 15.0, 5.0 / 12.0, 3.0 / 4.0)
TIME_STEP = 0.3
STREAM_SCALE = 2.0
SPAN_SCALE = 2.0
COUPLING = 0.5
CORNER_LIST = (
    (0, 0, 0),
    (0, 0, 1),
    (0, 1, 0),
    (0, 1, 1),
    (1, 0, 0),
    (1, 0, 1),
    (1, 1, 0),
    (1, 1, 1),
)


def carried_in(part, axis, combine, identity, reverse):
    count = lax.axis_size(axis)
    place = lax.axis_index(axis)
    ahead = count - 1 - place if reverse else place
    gathered = jax.tree.map(lambda a: lax.all_gather(a, axis), part)
    state = jax.tree.map(lambda a, e: jnp.zeros_like(a) + jnp.asarray(e, a.dtype), part, identity)

    def one(turn, state):
        source = count - 1 - turn if reverse else turn
        return combine(
            state, jax.tree.map(lambda a: lax.dynamic_index_in_dim(a, source, 0, False), gathered)
        )

    return lax.fori_loop(0, ahead, one, state)


def extended_2(x, sides, width, wrap):
    for axis, dim in sides:
        size, length = (lax.axis_size(axis), x.shape[dim])
        up = [(i, (i + 1) % size) for i in range(size if wrap else size - 1)]
        down = [(j, i) for i, j in up]
        last = lax.slice_in_dim(x, length - width, length, axis=dim)
        first = lax.slice_in_dim(x, 0, width, axis=dim)
        before = lax.ppermute(last, axis, up)
        after = lax.ppermute(first, axis, down)
        x = jnp.concatenate([before, x, after], axis=dim)
    return x


def from_behind(block, axis, distance):
    devices = range(lax.axis_size(axis))
    route = [((i - distance) % len(devices), i) for i in devices]
    return lax.ppermute(block, axis, route)


def stencil(field, upper_x, lower_x, upper_y, lower_y, upper_z, lower_z, y_metric):
    slope_x = (upper_x - lower_x) * (0.5 * STREAM_SCALE)
    slope_y = (upper_y - lower_y) * (0.5 * y_metric)[None, None, :, None]
    slope_z = (upper_z - lower_z) * (0.5 * SPAN_SCALE)
    return -(field[0:1] * slope_x + field[1:2] * slope_y + field[2:3] * slope_z)


def corner_weight(offsets, corner):
    weight = None
    for dimension in range(3):
        factor = offsets[dimension] if corner[dimension] else 1.0 - offsets[dimension]
        weight = factor if weight is None else weight * factor
    return weight


def chain(earlier, later):
    return (later[0] * earlier[0], later[0] * earlier[1] + later[1])


def carry_in(factor, offset, backward):
    identity = (jnp.ones_like(factor), jnp.zeros_like(offset))
    if backward:
        result = carried_in((factor, offset), "gy", chain, identity, True)
        return result[1]
    result = carried_in((factor, offset), "gy", chain, identity, False)
    return result[1]


def local_solve(rhs, down_rate, up_rate, scale_rate):
    rows = rhs.shape[2]
    order = jnp.arange(rows)
    growth = jnp.cumprod(down_rate)
    lower_table = jnp.where(
        order[:, None] >= order[None, :], growth[:, None] / growth[None, :], 0.0
    )
    partial_down = jnp.einsum("ji,cxiz->cxjz", lower_table, rhs, precision=lax.Precision.HIGHEST)
    entering = carry_in(growth[-1:].reshape(1, 1), partial_down[:, :, -1, :], False)
    forward = partial_down + growth[None, None, :, None] * entering[:, :, None, :]
    shrink = jnp.cumprod(up_rate[::-1])[::-1]
    upper_table = jnp.where(
        order[:, None] <= order[None, :], shrink[:, None] / shrink[None, :], 0.0
    )
    scaled = scale_rate[None, None, :, None] * forward
    partial_up = jnp.einsum("ji,cxiz->cxjz", upper_table, scaled, precision=lax.Precision.HIGHEST)
    leaving = carry_in(shrink[:1].reshape(1, 1), partial_up[:, :, 0, :], True)
    return partial_up + shrink[None, None, :, None] * leaving[:, :, None, :]


def on_device(
    velocity,
    y_metric,
    forward_rate,
    backward_rate,
    pivot_inv,
    particle_vel,
    particle_cell,
    particle_offset,
    inverse_tau,
    outgoing_count,
):
    comps, cells_x, cells_y, cells_z = velocity.shape
    slot_total = particle_vel.shape[1]
    counts = outgoing_count.reshape(3)
    slot_num = jnp.arange(slot_total)
    remain = slot_num - RESIDENT
    heading = jnp.clip(remain // CAP, 0, 2)
    limit = jnp.where(heading == 0, counts[0], jnp.where(heading == 1, counts[1], counts[2]))
    live = jnp.where((slot_num < RESIDENT) | (remain % CAP < limit), 1.0, 0.0).astype(jnp.float32)
    cell_x = particle_cell // (cells_y * cells_z)
    cell_y = particle_cell // cells_z % cells_y
    cell_z = particle_cell % cells_z
    lanes = lax.axis_size("gy")
    position = lax.axis_index("gy")
    row_order = jnp.arange(cells_y + 2)
    wall_rows = (row_order == 0) & (position == 0) | (row_order == cells_y + 1) & (
        position == lanes - 1
    )
    keep_rows = jnp.where(wall_rows, 0.0, 1.0)[None, None, :, None]
    field = velocity
    moving = particle_vel
    for section_num in range(SECTIONS):
        step_size = TIME_STEP * SECTION_WEIGHTS[section_num]
        extended = extended_2(field, (("gx", 1), ("gy", 2)), 1, True) * keep_rows
        flat_ext = extended.reshape(comps, -1)
        fluid_at = jnp.zeros_like(moving)
        for corner in CORNER_LIST:
            lookup = (
                (cell_x + 1 + corner[0]) * (cells_y + 2) + cell_y + 1 + corner[1]
            ) * cells_z + (cell_z + corner[2]) % cells_z
            fluid_at = fluid_at + corner_weight(particle_offset, corner) * flat_ext[:, lookup]
        drag = inverse_tau * (fluid_at - moving)
        moving = moving + step_size * drag
        force = (
            jnp.zeros((comps, cells_x * cells_y * cells_z), jnp.float32)
            .at[:, particle_cell]
            .add(-COUPLING * drag * live)
        )
        convection = stencil(
            field,
            extended[:, 2:, 1:-1, :],
            extended[:, :-2, 1:-1, :],
            extended[:, 1:-1, 2:, :],
            extended[:, 1:-1, :-2, :],
            jnp.roll(field, -1, axis=3),
            jnp.roll(field, 1, axis=3),
            y_metric,
        )
        rhs = field + step_size * (convection + force.reshape(field.shape))
        field = local_solve(
            rhs, forward_rate[section_num], backward_rate[section_num], pivot_inv[section_num]
        )
    masked = moving * live[None, :]
    kept = masked[:, :RESIDENT]
    to_x = masked[:, RESIDENT : RESIDENT + CAP]
    to_lower = masked[:, RESIDENT + CAP : RESIDENT + 2 * CAP]
    to_upper = masked[:, RESIDENT + 2 * CAP :]
    from_x = from_behind(to_x, "gx", 1)
    paired = jnp.stack([to_lower, to_upper], axis=1)
    arrived = extended_2(paired, (("gy", 1),), 1, False)
    moved = jnp.concatenate([kept, from_x, arrived[:, 3], arrived[:, 0]], axis=1)
    return (field, moved)


def solution(mesh):
    return jax.shard_map(
        on_device,
        mesh=mesh,
        in_specs=(
            P(None, "gx", "gy", None),
            P("gy"),
            P(None, "gy"),
            P(None, "gy"),
            P(None, "gy"),
            P(None, ("gx", "gy")),
            P(("gx", "gy")),
            P(None, ("gx", "gy")),
            P(("gx", "gy")),
            P("gx", "gy", None),
        ),
        out_specs=(P(None, "gx", "gy", None), P(None, ("gx", "gy"))),
        check_vma=False,
    )
```

profile of v0, /device:TPU:1, one launch (start us, length us, event | category | flops | bytes accessed | tf_op | source)
XLA Modules:
  0.0 1173.2 jit_solution(15181815401981372482)
XLA Ops:
  0.7 6.5 collective-permute-start.1
  44.7 66.0 %all-reduce.6 = (f32[32]{0:T(128)}, f32[32]{0:T(128)}, f32[32]{0:T(128)}, f32[32]{0:T(128)}, f32[32]{0:T(128)}, /*index=5*/f32[32]{0:T(128)}) all-reduce(f32[32]{0:T(128)S(1)} %bitcast_dynamic-update-slice_fusion.5, f32[32]{0:T(128)S(1)} %bitcast_dynamic-update-slice_fusion.4, ...), channel_id=2, replica_groups=mesh['gx'=8,'gy'=32] {'gy'}, use_global_device_ids=true, to_apply=%add | all-reduce | flops 192 | bytes 1536
  110.9 13.6 %copy.195 = f32[3,3,18,1024]{0,3,2,1:T(8,128)} copy(f32[3,3,18,1024]{3,2,0,1:T(8,128)S(1)} %get-tuple-element.489) | data formatting | bytes 1327104 | tf_op jit(solution)/shard_map/concatenate | solution.py:53
  124.5 25.9 %bitcast_multiply_fusion.2 = f32[3,55296]{0,1:T(8,128)} fusion(f32[3,3,18,1024]{0,3,2,1:T(8,128)} %copy.195, f32[55296]{0:T(1024)S(1)} %mul.898), kind=kLoop, calls=%fused_computation.41 | loop fusion | flops 165888 | bytes 1548288 | tf_op jit(solution)/shard_map/mul | solution.py:145
  150.4 15.7 %gather_fusion.7 = f32[3584,3]{1,0:T(8,128)S(1)} fusion(f32[3,55296]{0,1:T(8,128)} %bitcast_multiply_fusion.2, s32[4096]{0:T(1024)} %get-tuple-element.553), kind=kCustom, calls=%fused_computation.7 | custom fusion | bytes 100352 | tf_op jit(solution)/shard_map/gather | solution.py:152
  167.3 15.7 %gather_fusion.6 = f32[3584,3]{1,0:T(8,128)S(1)} fusion(f32[3,55296]{0,1:T(8,128)} %bitcast_multiply_fusion.2, s32[4096]{0:T(1024)} %get-tuple-element.554), kind=kCustom, calls=%fused_computation.6 | custom fusion | bytes 100352 | tf_op jit(solution)/shard_map/gather | solution.py:152
  184.2 15.7 %gather_fusion.5 = f32[3584,3]{1,0:T(8,128)S(1)} fusion(f32[3,55296]{0,1:T(8,128)} %bitcast_multiply_fusion.2, s32[4096]{0:T(1024)} %pad_clamp_fusion.2), kind=kCustom, calls=%fused_computation.5 | custom fusion | bytes 100352 | tf_op jit(solution)/shard_map/gather | solution.py:152
  201.1 15.7 %gather_fusion.4 = f32[3584,3]{1,0:T(8,128)S(1)} fusion(f32[3,55296]{0,1:T(8,128)} %bitcast_multiply_fusion.2, s32[4096]{0:T(1024)} %get-tuple-element.547), kind=kCustom, calls=%fused_computation.4 | custom fusion | bytes 100352 | tf_op jit(solution)/shard_map/gather | solution.py:152
  218.0 15.7 %gather_fusion.3 = f32[3584,3]{1,0:T(8,128)S(1)} fusion(f32[3,55296]{0,1:T(8,128)} %bitcast_multiply_fusion.2, s32[4096]{0:T(1024)} %get-tuple-element.548), kind=kCustom, calls=%fused_computation.3 | custom fusion | bytes 100352 | tf_op jit(solution)/shard_map/gather | solution.py:152
  234.9 15.7 %gather_fusion.2 = f32[3584,3]{1,0:T(8,128)S(1)} fusion(f32[3,55296]{0,1:T(8,128)} %bitcast_multiply_fusion.2, s32[4096]{0:T(1024)} %get-tuple-element.549), kind=kCustom, calls=%fused_computation.2 | custom fusion | bytes 100352 | tf_op jit(solution)/shard_map/gather | solution.py:152
  251.8 15.7 %gather_fusion.1 = f32[3584,3]{1,0:T(8,128)S(1)} fusion(f32[3,55296]{0,1:T(8,128)} %bitcast_multiply_fusion.2, s32[4096]{0:T(1024)} %get-tuple-element.550), kind=kCustom, calls=%fused_computation.1 | custom fusion | bytes 100352 | tf_op jit(solution)/shard_map/gather | solution.py:152
  268.6 14.8 %gather_fusion = f32[3584,3]{1,0:T(8,128)S(1)} fusion(f32[3,55296]{0,1:T(8,128)} %bitcast_multiply_fusion.2, s32[4096]{0:T(1024)S(1)} %pad_clamp_fusion.7), kind=kCustom, calls=%fused_computation | custom fusion | bytes 100352 | tf_op jit(solution)/shard_map/gather | solution.py:152
  287.9 23.6 %scatter_custom_fusion = f32[3,16384]{0,1:T(8,128)} fusion(s32[3584]{0:T(1024)} %get-tuple-element.534, f32[3584,3]{1,0:T(8,128)S(1)} %copy.155, f32[]{:T(128)} %constant.303.clone.1), kind=kCustom, calls=%fused_computation.46 | custom fusion | flops 10752 | bytes 197120 | tf_op jit(solution)/shard_map/scatter-add | solution.py:158
  311.5 5.3 copy.196
  317.4 27.7 %all-gather.1 = f32[96,1,1,1024]{3,2,1,0:T(1,128)S(1)} all-gather(f32[3,1,1,1024]{3,2,1,0:T(1,128)S(1)} %slice_bitcast_fusion.14), channel_id=3, replica_groups=mesh['gx'=8,'gy'=32] {'gy'}, dimensions={0}, use_global_device_ids=true | all-gather | bytes 405504 | tf_op jit(solution)/shard_map/all_gather | solution.py:32
  346.8 60.5 %all-gather.3 = f32[96,1,1,1024]{3,2,1,0:T(1,128)S(1)} all-gather(f32[3,1,1,1024]{3,2,1,0:T(1,128)S(1)} %slice_bitcast_fusion.13), channel_id=5, replica_groups=mesh['gx'=8,'gy'=32] {'gy'}, dimensions={0}, use_global_device_ids=true | all-gather | bytes 405504 | tf_op jit(solution)/shard_map/all_gather | solution.py:32
  407.3 38.3 %while.79 = (s32[]{:T(128)}, f32[3,1,1024]{2,1,0:T(1,128)S(1)}, s32[]{:T(128)}, f32[32,1,1]{0,2,1:T(1,128)S(1)}, f32[32,3,1,1024]{3,2,1,0:T(1,128)S(1)}, /*index=5*/s32[]{:T(128)}, s32[]{:T(128)}, s32[]{:T(128)}, s32[]{:T(128)}) while((s32[]{:T(128)}, f32[3,1,1024]{2,1,0:T(1,128)S(1)}, s32[]{:T(128)}, f32[32,1,1]{0,2,1:T(1,128)S(1)}, ...), condition=%wide.region_6.7_spmd, body=%wide.region_5.6_spmd.sunk | while | flops 6150 | bytes 37031 | solution.py:41
  454.3 2.9 collective-permute-start.7
  458.9 13.6 %copy.197 = f32[3,3,18,1024]{0,3,2,1:T(8,128)} copy(f32[3,3,18,1024]{3,2,0,1:T(8,128)S(1)} %get-tuple-element.487) | data formatting | bytes 1327104 | tf_op jit(solution)/shard_map/concatenate | solution.py:53
  472.5 26.0 %bitcast_multiply_fusion.1 = f32[3,55296]{0,1:T(8,128)} fusion(f32[3,3,18,1024]{0,3,2,1:T(8,128)} %copy.197, f32[55296]{0:T(1024)S(1)} %mul.898), kind=kLoop, calls=%fused_computation.40 | loop fusion | flops 165888 | bytes 1548288 | tf_op jit(solution)/shard_map/mul | solution.py:145
  498.5 16.4 %gather_fusion.15 = f32[3584,3]{1,0:T(8,128)} fusion(f32[3,55296]{0,1:T(8,128)} %bitcast_multiply_fusion.1, s32[4096]{0:T(1024)S(1)} %copy-done.16), kind=kCustom, calls=%fused_computation.15 | custom fusion | bytes 100352 | tf_op jit(solution)/shard_map/gather | solution.py:152
  514.9 16.4 %gather_fusion.14 = f32[3584,3]{1,0:T(8,128)} fusion(f32[3,55296]{0,1:T(8,128)} %bitcast_multiply_fusion.1, s32[4096]{0:T(1024)S(1)} %copy-done.10), kind=kCustom, calls=%fused_computation.14 | custom fusion | bytes 100352 | tf_op jit(solution)/shard_map/gather | solution.py:152
  531.4 16.4 %gather_fusion.13 = f32[3584,3]{1,0:T(8,128)} fusion(f32[3,55296]{0,1:T(8,128)} %bitcast_multiply_fusion.1, s32[4096]{0:T(1024)S(1)} %copy-done.6), kind=kCustom, calls=%fused_computation.13 | custom fusion | bytes 100352 | tf_op jit(solution)/shard_map/gather | solution.py:152
  547.8 16.4 %gather_fusion.12 = f32[3584,3]{1,0:T(8,128)} fusion(f32[3,55296]{0,1:T(8,128)} %bitcast_multiply_fusion.1, s32[4096]{0:T(1024)S(1)} %copy-done.12), kind=kCustom, calls=%fused_computation.12 | custom fusion | bytes 100352 | tf_op jit(solution)/shard_map/gather | solution.py:152
  564.2 16.4 %gather_fusion.11 = f32[3584,3]{1,0:T(8,128)} fusion(f32[3,55296]{0,1:T(8,128)} %bitcast_multiply_fusion.1, s32[4096]{0:T(1024)S(1)} %copy-done.8), kind=kCustom, calls=%fused_computation.11 | custom fusion | bytes 100352 | tf_op jit(solution)/shard_map/gather | solution.py:152
  580.6 16.4 %gather_fusion.10 = f32[3584,3]{1,0:T(8,128)} fusion(f32[3,55296]{0,1:T(8,128)} %bitcast_multiply_fusion.1, s32[4096]{0:T(1024)S(1)} %copy-done.18), kind=kCustom, calls=%fused_computation.10 | custom fusion | bytes 100352 | tf_op jit(solution)/shard_map/gather | solution.py:152
  597.0 16.4 %gather_fusion.9 = f32[3584,3]{1,0:T(8,128)} fusion(f32[3,55296]{0,1:T(8,128)} %bitcast_multiply_fusion.1, s32[4096]{0:T(1024)S(1)} %copy-done.14), kind=kCustom, calls=%fused_computation.9 | custom fusion | bytes 100352 | tf_op jit(solution)/shard_map/gather | solution.py:152
  613.4 14.8 %gather_fusion.8 = f32[3584,3]{1,0:T(8,128)S(1)} fusion(f32[3,55296]{0,1:T(8,128)} %bitcast_multiply_fusion.1, s32[4096]{0:T(1024)S(1)} %pad_clamp_fusion.7), kind=kCustom, calls=%fused_computation.8 | custom fusion | bytes 100352 | tf_op jit(solution)/shard_map/gather | solution.py:152
  651.2 23.6 %scatter_custom_fusion.1 = f32[3,16384]{0,1:T(8,128)} fusion(s32[3584]{0:T(1024)} %get-tuple-element.534, f32[3584,3]{1,0:T(8,128)S(1)} %copy.172, f32[]{:T(128)} %constant.303.clone.1), kind=kCustom, calls=%fused_computation.44 | custom fusion | flops 10752 | bytes 197120 | tf_op jit(solution)/shard_map/scatter-add | solution.py:158
  674.8 5.3 copy.198
  680.8 27.9 %all-gather.5 = f32[96,1,1,1024]{3,2,1,0:T(1,128)S(1)} all-gather(f32[3,1,1,1024]{3,2,1,0:T(1,128)S(1)} %slice_bitcast_fusion.12), channel_id=7, replica_groups=mesh['gx'=8,'gy'=32] {'gy'}, dimensions={0}, use_global_device_ids=true | all-gather | bytes 405504 | tf_op jit(solution)/shard_map/all_gather | solution.py:32
  710.4 60.5 %all-gather.7 = f32[96,1,1,1024]{3,2,1,0:T(1,128)S(1)} all-gather(f32[3,1,1,1024]{3,2,1,0:T(1,128)S(1)} %slice_bitcast_fusion.11), channel_id=9, replica_groups=mesh['gx'=8,'gy'=32] {'gy'}, dimensions={0}, use_global_device_ids=true | all-gather | bytes 405504 | tf_op jit(solution)/shard_map/all_gather | solution.py:32
  770.9 38.3 %while.81 = (s32[]{:T(128)}, f32[3,1,1024]{2,1,0:T(1,128)S(1)}, s32[]{:T(128)}, f32[32,1,1]{0,2,1:T(1,128)S(1)}, f32[32,3,1,1024]{3,2,1,0:T(1,128)S(1)}, /*index=5*/s32[]{:T(128)}, s32[]{:T(128)}, s32[]{:T(128)}, s32[]{:T(128)}) while((s32[]{:T(128)}, f32[3,1,1024]{2,1,0:T(1,128)S(1)}, s32[]{:T(128)}, f32[32,1,1]{0,2,1:T(1,128)S(1)}, ...), condition=%wide.region_13.14_spmd, body=%wide.region_12.13_spmd.sunk | while | flops 6150 | bytes 37031 | solution.py:41
  819.7 13.6 %copy.199 = f32[3,3,18,1024]{0,3,2,1:T(8,128)} copy(f32[3,3,18,1024]{3,2,0,1:T(8,128)S(1)} %get-tuple-element.485) | data formatting | bytes 1327104 | tf_op jit(solution)/shard_map/concatenate | solution.py:53
  833.3 26.0 %bitcast_multiply_fusion = f32[3,55296]{0,1:T(8,128)} fusion(f32[3,3,18,1024]{0,3,2,1:T(8,128)} %copy.199, f32[55296]{0:T(1024)S(1)} %mul.898), kind=kLoop, calls=%fused_computation.39 | loop fusion | flops 165888 | bytes 1548288 | tf_op jit(solution)/shard_map/mul | solution.py:145
  859.3 14.8 %gather_fusion.23 = f32[3584,3]{1,0:T(8,128)S(1)} fusion(f32[3,55296]{0,1:T(8,128)} %bitcast_multiply_fusion, s32[4096]{0:T(1024)S(1)} %copy-done.17), kind=kCustom, calls=%fused_computation.23 | custom fusion | bytes 100352 | tf_op jit(solution)/shard_map/gather | solution.py:152
  874.1 16.4 %gather_fusion.22 = f32[3584,3]{1,0:T(8,128)} fusion(f32[3,55296]{0,1:T(8,128)} %bitcast_multiply_fusion, s32[4096]{0:T(1024)S(1)} %copy-done.11), kind=kCustom, calls=%fused_computation.22 | custom fusion | bytes 100352 | tf_op jit(solution)/shard_map/gather | solution.py:152
  890.5 16.4 %gather_fusion.21 = f32[3584,3]{1,0:T(8,128)} fusion(f32[3,55296]{0,1:T(8,128)} %bitcast_multiply_fusion, s32[4096]{0:T(1024)S(1)} %copy-done.7), kind=kCustom, calls=%fused_computation.21 | custom fusion | bytes 100352 | tf_op jit(solution)/shard_map/gather | solution.py:152
  907.0 16.4 %gather_fusion.20 = f32[3584,3]{1,0:T(8,128)} fusion(f32[3,55296]{0,1:T(8,128)} %bitcast_multiply_fusion, s32[4096]{0:T(1024)S(1)} %copy-done.13), kind=kCustom, calls=%fused_computation.20 | custom fusion | bytes 100352 | tf_op jit(solution)/shard_map/gather | solution.py:152
  923.4 16.4 %gather_fusion.19 = f32[3584,3]{1,0:T(8,128)} fusion(f32[3,55296]{0,1:T(8,128)} %bitcast_multiply_fusion, s32[4096]{0:T(1024)S(1)} %copy-done.9), kind=kCustom, calls=%fused_computation.19 | custom fusion | bytes 100352 | tf_op jit(solution)/shard_map/gather | solution.py:152
  939.8 16.4 %gather_fusion.18 = f32[3584,3]{1,0:T(8,128)} fusion(f32[3,55296]{0,1:T(8,128)} %bitcast_multiply_fusion, s32[4096]{0:T(1024)S(1)} %copy-done.19), kind=kCustom, calls=%fused_computation.18 | custom fusion | bytes 100352 | tf_op jit(solution)/shard_map/gather | solution.py:152
  956.2 16.4 %gather_fusion.17 = f32[3584,3]{1,0:T(8,128)} fusion(f32[3,55296]{0,1:T(8,128)} %bitcast_multiply_fusion, s32[4096]{0:T(1024)S(1)} %copy-done.15), kind=kCustom, calls=%fused_computation.17 | custom fusion | bytes 100352 | tf_op jit(solution)/shard_map/gather | solution.py:152
  972.6 16.4 %gather_fusion.16 = f32[3584,3]{1,0:T(8,128)} fusion(f32[3,55296]{0,1:T(8,128)} %bitcast_multiply_fusion, s32[4096]{0:T(1024)S(1)} %pad_clamp_fusion.7), kind=kCustom, calls=%fused_computation.16 | custom fusion | bytes 100352 | tf_op jit(solution)/shard_map/gather | solution.py:152
  1006.0 23.6 %scatter_custom_fusion.2 = f32[3,16384]{0,1:T(8,128)} fusion(s32[3584]{0:T(1024)} %get-tuple-element.534, f32[3584,3]{1,0:T(8,128)S(1)} %copy.188, f32[]{:T(128)} %constant.303.clone.1), kind=kCustom, calls=%fused_computation.42 | custom fusion | flops 10752 | bytes 197120 | tf_op jit(solution)/shard_map/scatter-add | solution.py:158
  1029.6 5.3 copy.200
  1035.5 27.6 %all-gather.9 = f32[96,1,1,1024]{3,2,1,0:T(1,128)S(1)} all-gather(f32[3,1,1,1024]{3,2,1,0:T(1,128)S(1)} %slice_bitcast_fusion.10), channel_id=11, replica_groups=mesh['gx'=8,'gy'=32] {'gy'}, dimensions={0}, use_global_device_ids=true | all-gather | bytes 405504 | tf_op jit(solution)/shard_map/all_gather | solution.py:32
  1064.9 60.5 %all-gather.11 = f32[96,1,1,1024]{3,2,1,0:T(1,128)S(1)} all-gather(f32[3,1,1,1024]{3,2,1,0:T(1,128)S(1)} %slice_bitcast_fusion.9), channel_id=13, replica_groups=mesh['gx'=8,'gy'=32] {'gy'}, dimensions={0}, use_global_device_ids=true | all-gather | bytes 405504 | tf_op jit(solution)/shard_map/all_gather | solution.py:32
  1125.4 38.3 %while.83 = (s32[]{:T(128)}, f32[3,1,1024]{2,1,0:T(1,128)S(1)}, s32[]{:T(128)}, f32[32,1,1]{0,2,1:T(1,128)S(1)}, f32[32,3,1,1024]{3,2,1,0:T(1,128)S(1)}, /*index=5*/s32[]{:T(128)}, s32[]{:T(128)}, s32[]{:T(128)}, s32[]{:T(128)}) while((s32[]{:T(128)}, f32[3,1,1024]{2,1,0:T(1,128)S(1)}, s32[]{:T(128)}, f32[32,1,1]{0,2,1:T(1,128)S(1)}, ...), condition=%wide.region_20.21_spmd, body=%wide.region_19.20_spmd.sunk | while | flops 6150 | bytes 37031 | solution.py:41
  (504 shorter events, 243.2 us)
Async XLA Ops:
  0.6 25.5 %copy-start = (f32[3,1,16,1024]{3,2,1,0:T(8,128)S(1)}, f32[3,1,16,1024]{3,2,1,0:T(8,128)}, u32[]{:S(2)}) copy-start(f32[3,1,16,1024]{3,2,1,0:T(8,128)} %param.22) | copy-start | bytes 589828
  0.6 24.9 %copy-start.67 = (f32[16]{0:T(128)S(1)}, f32[16]{0:T(128)}, u32[]{:S(2)}) copy-start(f32[16]{0:T(128)} %param.23) | copy-start | bytes 196
  0.7 25.5 %collective-permute-start.1 = (f32[3,1,16,1024]{3,2,0,1:T(8,128)}, f32[3,1,16,1024]{3,2,0,1:T(8,128)S(1)}, u32[]{:S(2)}, u32[]{:S(2)}) collective-permute-start(f32[3,1,16,1024]{3,2,0,1:T(8,128)} %bitcast.267), channel_id=1, source_target_pairs={{32,0},{64,32},{96,64},{128,96},{160,128},{192,160},{224,192},{0,2... | collective-permute-start | bytes 589832 | tf_op jit(solution)/shard_map/ppermute | solution.py:52
  7.1 19.0 %collective-permute-start = (f32[3,1,16,1024]{3,2,0,1:T(8,128)}, f32[3,1,16,1024]{3,2,0,1:T(8,128)S(1)}, u32[]{:S(2)}, u32[]{:S(2)}) collective-permute-start(f32[3,1,16,1024]{3,2,0,1:T(8,128)} %bitcast.268), channel_id=1, source_target_pairs={{0,32},{32,64},{64,96},{96,128},{128,160},{160,192},{192,224},{224... | collective-permute-start | bytes 589832 | tf_op jit(solution)/shard_map/ppermute | solution.py:51
  8.6 27.4 %copy-start.74 = (u32[256]{0:T(256)S(1)}, u32[256]{0:T(256)}, u32[]{:S(2)}) copy-start(u32[256]{0:T(256)} %constant.336) | copy-start | bytes 3076
  26.2 84.5 %collective-permute-start.3 = (f32[3,3,1,1024]{3,2,0,1:T(1,128)S(1)}, f32[3,3,1,1024]{3,2,0,1:T(1,128)S(1)}, u32[]{:S(2)}, u32[]{:S(2)}) collective-permute-start(f32[3,3,1,1024]{3,2,0,1:T(1,128)S(1)} %get-tuple-element.495), channel_id=1, source_target_pairs={{1,0},{2,1},{3,2},{4,3},{5,4},{6,5},{7,6},{8,7},{9,8},{10,9},{11,1... | collective-permute-start | bytes 110600 | tf_op jit(solution)/shard_map/ppermute | solution.py:52
  27.2 83.4 %collective-permute-start.2 = (f32[3,3,1,1024]{3,2,0,1:T(1,128)S(1)}, f32[3,3,1,1024]{3,2,0,1:T(1,128)S(1)}, u32[]{:S(2)}, u32[]{:S(2)}) collective-permute-start(f32[3,3,1,1024]{3,2,0,1:T(1,128)S(1)} %get-tuple-element.494), channel_id=1, source_target_pairs={{0,1},{1,2},{2,3},{3,4},{4,5},{5,6},{6,7},{7,8},{8,9},{9,10},{10,1... | collective-permute-start | bytes 110600 | tf_op jit(solution)/shard_map/ppermute | solution.py:51
  28.4 96.1 %copy-start.55 = (f32[18]{0:T(128)}, f32[18]{0:T(128)S(1)}, u32[]{:S(2)}) copy-start(f32[18]{0:T(128)S(1)} %or_select_fusion) | copy-start | bytes 220
  316.8 28.3 %copy-start.73 = (f32[32]{0:T(128)S(1)}, f32[32]{0:T(128)}, u32[]{:S(2)}) copy-start(f32[32]{0:T(128)} %get-tuple-element.468) | copy-start | bytes 388
  316.8 29.6 %copy-start.63 = (f32[16]{0:T(128)S(1)}, f32[16]{0:T(128)}, u32[]{:S(2)}) copy-start(f32[16]{0:T(128)} %rev.19) | copy-start | bytes 196
  316.8 29.6 %copy-start.66 = (f32[16]{0:T(128)S(1)}, f32[16]{0:T(128)}, u32[]{:S(2)}) copy-start(f32[16]{0:T(128)} %get-tuple-element.536) | copy-start | bytes 196
  316.8 90.5 %copy-start.72 = (f32[32]{0:T(128)S(1)}, f32[32]{0:T(128)}, u32[]{:S(2)}) copy-start(f32[32]{0:T(128)} %get-tuple-element.469) | copy-start | bytes 388
  346.4 112.2 %copy-start.56 = (f32[18]{0:T(128)S(1)}, f32[18]{0:T(128)}, u32[]{:S(2)}) copy-start(f32[18]{0:T(128)} %copy-done.55) | copy-start | bytes 220
  445.7 5.6 collective-permute-start.5
  448.5 5.7 collective-permute-start.4
  454.3 3.9 collective-permute-start.7
  457.2 1.4 collective-permute-start.6
  472.5 26.0 %copy-start.16 = (s32[4096]{0:T(1024)S(1)}, s32[4096]{0:T(1024)}, u32[]{:S(2)}) copy-start(s32[4096]{0:T(1024)} %get-tuple-element.553) | copy-start | bytes 49156
  472.5 42.5 %copy-start.10 = (s32[4096]{0:T(1024)S(1)}, s32[4096]{0:T(1024)}, u32[]{:S(2)}) copy-start(s32[4096]{0:T(1024)} %get-tuple-element.554) | copy-start | bytes 49156
  472.5 58.9 %copy-start.6 = (s32[4096]{0:T(1024)S(1)}, s32[4096]{0:T(1024)}, u32[]{:S(2)}) copy-start(s32[4096]{0:T(1024)} %pad_clamp_fusion.2) | copy-start | bytes 49156
  472.5 75.3 %copy-start.12 = (s32[4096]{0:T(1024)S(1)}, s32[4096]{0:T(1024)}, u32[]{:S(2)}) copy-start(s32[4096]{0:T(1024)} %get-tuple-element.547) | copy-start | bytes 49156
  498.5 65.7 %copy-start.8 = (s32[4096]{0:T(1024)S(1)}, s32[4096]{0:T(1024)}, u32[]{:S(2)}) copy-start(s32[4096]{0:T(1024)} %get-tuple-element.548) | copy-start | bytes 49156
  498.5 82.1 %copy-start.18 = (s32[4096]{0:T(1024)S(1)}, s32[4096]{0:T(1024)}, u32[]{:S(2)}) copy-start(s32[4096]{0:T(1024)} %get-tuple-element.549) | copy-start | bytes 49156
  498.5 98.5 %copy-start.14 = (s32[4096]{0:T(1024)S(1)}, s32[4096]{0:T(1024)}, u32[]{:S(2)}) copy-start(s32[4096]{0:T(1024)} %get-tuple-element.550) | copy-start | bytes 49156
  680.1 28.5 %copy-start.71 = (f32[32]{0:T(128)S(1)}, f32[32]{0:T(128)}, u32[]{:S(2)}) copy-start(f32[32]{0:T(128)} %get-tuple-element.470) | copy-start | bytes 388
  680.2 29.8 %copy-start.62 = (f32[16]{0:T(128)S(1)}, f32[16]{0:T(128)}, u32[]{:S(2)}) copy-start(f32[16]{0:T(128)} %rev.21) | copy-start | bytes 196
  680.2 29.8 %copy-start.65 = (f32[16]{0:T(128)S(1)}, f32[16]{0:T(128)}, u32[]{:S(2)}) copy-start(f32[16]{0:T(128)} %get-tuple-element.537) | copy-start | bytes 196
  680.2 90.7 %copy-start.70 = (f32[32]{0:T(128)S(1)}, f32[32]{0:T(128)}, u32[]{:S(2)}) copy-start(f32[32]{0:T(128)} %get-tuple-element.471) | copy-start | bytes 388
  710.0 109.5 %copy-start.57 = (f32[18]{0:T(128)S(1)}, f32[18]{0:T(128)}, u32[]{:S(2)}) copy-start(f32[18]{0:T(128)} %copy-done.55) | copy-start | bytes 220
  809.3 5.1 collective-permute-start.9
  809.4 6.2 collective-permute-start.8
  815.6 3.5 collective-permute-start.11
  818.1 1.4 collective-permute-start.10
  833.3 26.0 %copy-start.17 = (s32[4096]{0:T(1024)S(1)}, s32[4096]{0:T(1024)}, u32[]{:S(2)}) copy-start(s32[4096]{0:T(1024)} %get-tuple-element.553) | copy-start | bytes 49156
  833.3 40.8 %copy-start.11 = (s32[4096]{0:T(1024)S(1)}, s32[4096]{0:T(1024)}, u32[]{:S(2)}) copy-start(s32[4096]{0:T(1024)} %get-tuple-element.554) | copy-start | bytes 49156
  833.3 57.2 %copy-start.7 = (s32[4096]{0:T(1024)S(1)}, s32[4096]{0:T(1024)}, u32[]{:S(2)}) copy-start(s32[4096]{0:T(1024)} %pad_clamp_fusion.2) | copy-start | bytes 49156
  833.3 73.7 %copy-start.13 = (s32[4096]{0:T(1024)S(1)}, s32[4096]{0:T(1024)}, u32[]{:S(2)}) copy-start(s32[4096]{0:T(1024)} %get-tuple-element.547) | copy-start | bytes 49156
  859.3 64.1 %copy-start.9 = (s32[4096]{0:T(1024)S(1)}, s32[4096]{0:T(1024)}, u32[]{:S(2)}) copy-start(s32[4096]{0:T(1024)} %get-tuple-element.548) | copy-start | bytes 49156
  859.3 80.5 %copy-start.19 = (s32[4096]{0:T(1024)S(1)}, s32[4096]{0:T(1024)}, u32[]{:S(2)}) copy-start(s32[4096]{0:T(1024)} %get-tuple-element.549) | copy-start | bytes 49156
  859.3 96.9 %copy-start.15 = (s32[4096]{0:T(1024)S(1)}, s32[4096]{0:T(1024)}, u32[]{:S(2)}) copy-start(s32[4096]{0:T(1024)} %get-tuple-element.550) | copy-start | bytes 49156
  1034.9 28.3 %copy-start.69 = (f32[32]{0:T(128)S(1)}, f32[32]{0:T(128)}, u32[]{:S(2)}) copy-start(f32[32]{0:T(128)} %get-tuple-element.472) | copy-start | bytes 388
  1034.9 29.6 %copy-start.58 = (f32[16]{0:T(128)S(1)}, f32[16]{0:T(128)}, u32[]{:S(2)}) copy-start(f32[16]{0:T(128)} %rev.23) | copy-start | bytes 196
  1034.9 29.6 %copy-start.64 = (f32[16]{0:T(128)S(1)}, f32[16]{0:T(128)}, u32[]{:S(2)}) copy-start(f32[16]{0:T(128)} %get-tuple-element.535) | copy-start | bytes 196
  1034.9 90.4 %copy-start.68 = (f32[32]{0:T(128)S(1)}, f32[32]{0:T(128)}, u32[]{:S(2)}) copy-start(f32[32]{0:T(128)} %get-tuple-element.473) | copy-start | bytes 388
  1034.9 128.8 %copy-start.37 = (f32[3,3584]{1,0:T(4,128)S(1)}, f32[3,3584]{1,0:T(4,128)}, u32[]{:S(2)}) copy-start(f32[3,3584]{1,0:T(4,128)} %get-tuple-element.474) | copy-start | bytes 129028
  1163.7 5.7 collective-permute-start.14
  1165.7 5.0 collective-permute-start.13
  1168.4 3.9 collective-permute-start.12
  (42 other events, 164.3 us)
where the time goes:
time: 1180 us; the launch traced here: 1170 us
  local copies, waits for them, and re-layouts  570 us (48%)
  blocking collectives  331 us (28%)
  other arithmetic  229 us (19%)
  starting transfers between devices  23.7 us (2%)
  waiting for transfers between devices  12.8 us (1%)
    gather x48, local copies, waits for them, and re-layouts, on_device(): flat_ext[:, lookup]  428 us
    all_gather x6, blocking collectives, carried_in(): gathered = jax.tree.map(lambda a: lax.all_gather(a, axis), part)  265 us
    mul x6, other arithmetic, on_device(): extended = extended_2(field, (('gx', 1), ('gy', 2)), 1, True) * keep_rows  78.5 us
    scatter-add x3, other arithmetic, on_device(): force = jnp.zeros((comps, cells_x * cells_y * cells_z), jnp.float32).at[:...  70.7 us
    unnamed x1, blocking collectives  66 us
    add x93, other arithmetic, chain(): return (later[0] * earlier[0], later[0] * earlier[1] + later[1])  62.1 us
    dynamic_slice x93, local copies, waits for them, and re-layouts, one(): lax.dynamic_index_in_dim(a, source, 0, False)  54.4 us
    concatenate x3, local copies, waits for them, and re-layouts, extended_2(): x = jnp.concatenate([before, x, after], axis=dim)  40.8 us
  transfers between devices with their start and end apart: 15, of which 9 were waited for; matrix products, arithmetic and copies ran while one was open for 3% of the time, Pallas kernels for 0%

commit v1 on v0

v1 whole, which is shorter than its diff:
```python
import functools

import jax
import jax.numpy as jnp
from jax import lax
from jax.experimental import pallas as pl
from jax.experimental.pallas import tpu as pltpu
from jax.sharding import PartitionSpec as P

RESIDENT = 2048
CAP = 512
SECTIONS = 3
SECTION_WEIGHTS = (8.0 / 15.0, 5.0 / 12.0, 3.0 / 4.0)
TIME_STEP = 0.3
STREAM_SCALE = 2.0
SPAN_SCALE = 2.0
COUPLING = 0.5
CHUNK = 512
MESH = pl.DeviceIdType.MESH
F32 = jnp.float32
BF16 = jnp.bfloat16


def row_size(lanes):
    return 8 if lanes == 32 else max(2, lanes // 2)


def halves(x):
    high = x.astype(BF16)
    return high, (x - high.astype(F32)).astype(BF16)


def kernel(
    dims,
    vel, metric, fwd, bwd, piv, pvel, cell, offset, tau, count,
    field_out, part_out,
    onehot, table, el_table, scat, accum, wts, ymask, ywt, ab, speed, fluid, live_ref, moved,
    solve_cols, carry_col, alpha, beta, ymet, unit_rows,
    part, planes, uref, rhs_ref, edge, edge_in, msg, got1, got2, own2, ans, el, mig,
    s1s, s1r, s2s, s2r, s3s, s3r, pls, plr, eds, edr, mgs, mgr,
):
    nx, lanes, rsize = dims
    rows_n = lanes // rsize
    comps, cy, cz = vel.shape
    width = cz // rsize
    slots = pvel.shape[1]
    chunk = min(CHUNK, slots)
    steps = slots // chunk
    last = cy - 1
    gx = lax.axis_index("gx")
    gy = lax.axis_index("gy")
    place = lax.rem(gy, rsize)
    line = gy // rsize
    line0 = line * rsize
    west = lax.rem(gx + nx - 1, nx)
    east = lax.rem(gx + 1, nx)
    south = lax.rem(gy + lanes - 1, lanes)
    north = lax.rem(gy + 1, lanes)

    def send(src, dst, ssem, rsem, to):
        copy = pltpu.make_async_remote_copy(
            src_ref=src, dst_ref=dst, send_sem=ssem, recv_sem=rsem,
            device_id=to, device_id_type=MESH,
        )
        copy.start()
        return copy

    partners = []
    for d in range(1, rsize):
        partners.append((gx, line0 + lax.rem(place + d, rsize)))
    for d in range(1, rows_n):
        partners.append((gx, lax.rem(line + d, rows_n) * rsize + place))
    for d in range(rsize):
        mate = line0 + lax.rem(place + d, rsize)
        partners.append((west, mate))
        partners.append((east, mate))
    partners += [(gx, south), (gx, north), (west, south), (east, north)]
    barrier = pltpu.get_barrier_semaphore()
    for to in partners:
        pl.semaphore_signal(barrier, inc=1, device_id=to, device_id_type=MESH)

    for c in range(comps):
        edge[c : c + 1, :] = vel[c, last : last + 1, :]
        edge[3 + c : 4 + c, :] = vel[c, 0:1, :]
    edge[6:8, :] = jnp.zeros((2, cz), F32)
    for n, value in enumerate((piv[0, last], bwd[0, last], piv[1, last], bwd[1, last])):
        edge[6:7, n * 128 : (n + 1) * 128] = jnp.full((1, 128), value, F32)

    pl.semaphore_wait(barrier, len(partners))

    pending = []

    def send_planes(k, src):
        a = send(src, planes.at[k, 1], pls.at[k, 0], plr.at[k, 0], (west, gy))
        b = send(src, planes.at[k, 0], pls.at[k, 1], plr.at[k, 1], (east, gy))
        pending.extend([a, b])
        return a, b

    plane_copies = send_planes(0, vel)
    edge_copies = [
        send(edge, edge_in.at[0], eds.at[0], edr.at[0], (gx, north)),
        send(edge, edge_in.at[1], eds.at[1], edr.at[1], (gx, south)),
        send(edge, edge_in.at[2], eds.at[2], edr.at[2], (west, south)),
    ]
    pending.extend(edge_copies)

    row16 = lax.broadcasted_iota(jnp.int32, (cy, chunk), 0)
    lane = lax.broadcasted_iota(jnp.int32, (1, chunk), 1)
    zblock = min(256, cz)
    zrow = lax.broadcasted_iota(jnp.int32, (zblock, chunk), 0)
    c0, c1, c2 = count[0], count[1], count[2]
    speed[...] = jnp.zeros_like(speed)
    fluid[...] = jnp.zeros_like(fluid)

    def prepare(i, _):
        at = pl.ds(pl.multiple_of(i * chunk, chunk), chunk)
        where = cell[:, at]
        zpos = lax.rem(where, cz)
        ypos = lax.rem(lax.div(where, cz), cy)
        for n in range(cz // zblock):
            onehot[n * zblock : (n + 1) * zblock, at] = jnp.where(
                zrow + n * zblock == zpos, 1.0, 0.0
            ).astype(BF16)
        ox, oy, oz = offset[0:1, at], offset[1:2, at], offset[2:3, at]
        here = row16 == ypos
        above = row16 == ypos + 1
        ymask[:, at] = jnp.where(here, 1.0, 0.0)
        ywt[:, at] = jnp.where(here, 1.0 - oy, jnp.where(above, oy, 0.0))
        wts[0:1, at] = (1.0 - ox) * (1.0 - oz)
        wts[1:2, at] = (1.0 - ox) * oz
        wts[2:3, at] = ox * (1.0 - oz)
        wts[3:4, at] = ox * oz
        wts[4:5, at] = jnp.where(ypos == last, oy, 0.0)
        slot = lane + i * chunk
        out = slot - RESIDENT
        turn = jnp.where(out < CAP, out, jnp.where(out < 2 * CAP, out - CAP, out - 2 * CAP))
        limit = jnp.where(out < CAP, c0, jnp.where(out < 2 * CAP, c1, c2))
        live_ref[:, at] = jnp.where((out < 0) | (turn < limit), 1.0, 0.0)
        speed[0:3, at] = pvel[:, at]
        return 0

    lax.fori_loop(0, steps, prepare, 0)

    lane128 = lax.broadcasted_iota(jnp.int32, (1, 128), 1)
    for k in range(SECTIONS):
        g = jnp.zeros((1, 128), F32)
        gs = []
        for j in range(cy):
            g = jnp.where(lane128 == j, 1.0, 0.0) + fwd[k, j] * g
            gs.append(g)
        u = jnp.zeros((1, 128), F32)
        for j in reversed(range(cy)):
            u = piv[k, j] * gs[j] + bwd[k, j] * u
            unit_rows[j : j + 1, :] = u
        block = unit_rows[...]
        for i in range(cy):
            solve_cols[k, i] = jnp.broadcast_to(block[:, i : i + 1], (cy, 128))
        alpha[k] = jnp.broadcast_to(block[:, 0:1] * fwd[k, 0], (cy, cz))
        weight = jnp.float32(1.0)
        shrink = jnp.float32(1.0)
        for j in reversed(range(cy)):
            carry_col[k, j : j + 1, :] = jnp.full((1, 128), weight, F32)
            weight = weight * fwd[k, j]
            shrink = shrink * bwd[k, j]
            beta[k, j : j + 1, :] = jnp.full((1, cz), shrink, F32)
        for t in range(rsize):
            msg[k, t, 6:7, :] = jnp.full((1, width), weight, F32)
            half = lax.broadcasted_iota(jnp.int32, (1, width), 1) < width // 2
            msg[k, t, 7:8, :] = jnp.where(half, alpha[k, 0:1, 0:width], shrink)
    for j in range(cy):
        ymet[j : j + 1, :] = jnp.full((1, cz), 0.5 * metric[j], F32)

    def responses(i, _):
        at = pl.ds(pl.multiple_of(i * chunk, chunk), chunk)
        top = wts[4:5, at]
        w = ywt[:, at]
        zero = jnp.zeros((3, chunk), F32)
        two = jnp.zeros((2, chunk), F32)
        ab[0, :, at] = jnp.concatenate([zero, top, top, top, two], axis=0)
        for k in range(1, SECTIONS):
            a = jnp.sum(w * alpha[k - 1, :, 0:1], axis=0, keepdims=True)
            b = jnp.sum(w * beta[k - 1, :, 0:1], axis=0, keepdims=True) + top
            ab[k, :, at] = jnp.concatenate([a, a, a, b, b, b, two], axis=0)
        return 0

    lax.fori_loop(0, steps, responses, 0)

    def gather_plane(source, side):
        for c in range(comps):
            x = source[c]
            high, low = halves(x)
            table[0, c * cy : (c + 1) * cy, :] = high
            table[1, c * cy : (c + 1) * cy, :] = low
            high, low = halves(pltpu.roll(x, cz - 1, 1))
            at = (comps + c) * cy
            table[0, at : at + cy, :] = high
            table[1, at : at + cy, :] = low

        def one(i, _):
            at = pl.ds(pl.multiple_of(i * chunk, chunk), chunk)
            hot = onehot[:, at]
            got = jnp.dot(table[0], hot, preferred_element_type=F32) + jnp.dot(
                table[1], hot, preferred_element_type=F32
            )
            w0 = wts[2 * side : 2 * side + 1, at]
            w1 = wts[2 * side + 1 : 2 * side + 2, at]
            w = ywt[:, at]
            rows = []
            for c in range(comps):
                near = got[c * cy : (c + 1) * cy]
                far = got[(comps + c) * cy : (comps + c + 1) * cy]
                rows.append(jnp.sum((w0 * near + w1 * far) * w, axis=0, keepdims=True))
            value = jnp.concatenate(rows, axis=0)
            if side == 0:
                fluid[0:3, at] = value
            else:
                fluid[0:3, at] = fluid[0:3, at] + value
            return 0

        lax.fori_loop(0, steps, one, 0)

    sub = lax.broadcasted_iota(jnp.int32, (8, width), 0)
    col = lax.broadcasted_iota(jnp.int32, (8, width), 1)

    def coefficients(x):
        grow = jnp.broadcast_to(x[6:7], (8, width))
        seven = jnp.broadcast_to(x[7:8], (8, width))
        other = pltpu.roll(seven, width // 2, 1)
        mixed = jnp.where(col < width // 2, seven, other)
        shrink = jnp.where(col < width // 2, other, seven)
        return grow, mixed, shrink

    def lifted(e):
        return jnp.where((sub >= 3) & (sub < 6), pltpu.roll(e, 3, 0), jnp.where(sub == 6, e, 0.0))

    def down(x, grow, e):
        return jnp.where(sub < 3, x, 0.0) + grow * e

    def up(x, mixed, shrink, e, l):
        return jnp.where((sub >= 3) & (sub < 6), x, 0.0) + mixed * lifted(e) + shrink * l

    def plane_rows(k, slot):
        return jnp.concatenate([el[k, slot, t] for t in range(rsize)], axis=1)

    below_edge = jnp.where(gy > 0, 1.0, 0.0).astype(F32)
    above_edge = jnp.where(gy < lanes - 1, 1.0, 0.0).astype(F32)

    gather_plane(vel, 0)
    for copy in edge_copies:
        copy.wait_recv()
    for copy in plane_copies:
        copy.wait_recv()
    gather_plane(planes.at[0, 1], 1)

    for k in range(SECTIONS):
        step = TIME_STEP * SECTION_WEIGHTS[k]
        if k == 0:
            sub_full = lax.broadcasted_iota(jnp.int32, (8, cz), 0)
            upper = jnp.where((sub_full >= 3) & (sub_full < 6), 1.0, 0.0) * above_edge
            lower = jnp.where(sub_full < 3, 1.0, 0.0) * below_edge
            own = edge_in[0] * lower + edge_in[1] * upper
            plus = edge_in[2] * upper
            minus = None
        else:
            own, minus, plus = plane_rows(k - 1, 0), plane_rows(k - 1, 1), plane_rows(k - 1, 2)
        pair = jnp.concatenate([own, plus], axis=0)
        high, low = halves(pair)
        el_table[0, 0:16, :] = high
        el_table[1, 0:16, :] = low
        high, low = halves(pltpu.roll(pair, cz - 1, 1))
        el_table[0, 16:32, :] = high
        el_table[1, 16:32, :] = low

        def push(i, _, k=k, step=step):
            at = pl.ds(pl.multiple_of(i * chunk, chunk), chunk)
            hot = onehot[:, at]
            got = jnp.dot(el_table[0], hot, preferred_element_type=F32) + jnp.dot(
                el_table[1], hot, preferred_element_type=F32
            )
            mix = (
                wts[0:1, at] * got[0:8]
                + wts[2:3, at] * got[8:16]
                + wts[1:2, at] * got[16:24]
                + wts[3:4, at] * got[24:32]
            ) * ab[k, :, at]
            flow = fluid[:, at] + mix + pltpu.roll(mix, 5, 0)
            now = speed[:, at]
            drag = tau[:, at] * (flow - now)
            speed[:, at] = now + step * drag
            share = drag * (-COUPLING * live_ref[:, at])
            mask = ymask[:, at]
            for c in range(comps):
                one = share[c : c + 1]
                head = one.astype(BF16).astype(F32)
                scat[c * cy : (c + 1) * cy, at] = (mask * head).astype(BF16)
                scat[(comps + c) * cy : (comps + c + 1) * cy, at] = (mask * (one - head)).astype(BF16)
            return 0

        lax.fori_loop(0, steps, push, 0)

        if k == SECTIONS - 1:
            moved[...] = speed[...] * live_ref[...]
            trips = [
                send(moved.at[:, RESIDENT : RESIDENT + CAP], mig.at[0], mgs.at[0], mgr.at[0], (east, gy)),
                send(moved.at[:, RESIDENT + CAP : RESIDENT + 2 * CAP], mig.at[1], mgs.at[1], mgr.at[1], (gx, south)),
                send(moved.at[:, RESIDENT + 2 * CAP : RESIDENT + 3 * CAP], mig.at[2], mgs.at[2], mgr.at[2], (gx, north)),
            ]
            pending.extend(trips)

        def gathered(n, _):
            at = pl.ds(pl.multiple_of(n * zblock, zblock), zblock)
            both = lax.dot_general(
                scat[...], onehot[at, :], (((1,), (1,)), ((), ())), preferred_element_type=F32
            )
            half = comps * cy
            accum[:, at] = both[0:half] + both[half : 2 * half]
            return 0

        lax.fori_loop(0, cz // zblock, gathered, 0)

        def plane(source, c, rows):
            if k == 0:
                return source[c]
            return source[c] + alpha[k - 1] * rows[c : c + 1] + beta[k - 1] * rows[3 + c : 4 + c]

        for c in range(comps):
            uref[c] = plane(vel if k == 0 else part.at[k - 1], c, own)
        rowz = lax.broadcasted_iota(jnp.int32, (cy, cz), 0)
        for c in range(comps):
            u = uref[c]
            slope_x = (plane(planes.at[k, 1], c, plus) - plane(planes.at[k, 0], c, minus)) * (
                0.5 * STREAM_SCALE
            )
            slope_z = (pltpu.roll(u, cz - 1, 1) - pltpu.roll(u, 1, 1)) * (0.5 * SPAN_SCALE)
            if k == 0:
                under = own[c : c + 1]
            else:
                rate = edge_in[0, 6:7, :]
                base = 256 * (k - 1)
                pv = jnp.concatenate([rate[:, base : base + 128]] * (cz // 128), axis=1)
                bv = jnp.concatenate([rate[:, base + 128 : base + 256]] * (cz // 128), axis=1)
                under = (pv * own[c : c + 1] + bv * u[0:1]) * below_edge
            upper_y = jnp.where(rowz == last, own[3 + c : 4 + c], pltpu.roll(u, cy - 1, 0))
            lower_y = jnp.where(rowz == 0, under, pltpu.roll(u, 1, 0))
            slope_y = (upper_y - lower_y) * ymet[...]
            convection = -(uref[0] * slope_x + uref[1] * slope_y + uref[2] * slope_z)
            rhs_ref[c] = u + step * (convection + accum[c * cy : (c + 1) * cy, :])

        for c in range(comps):
            for z in range(cz // 128):
                at = slice(z * 128, (z + 1) * 128)
                total = None
                for i in range(cy):
                    term = solve_cols[k, i] * rhs_ref[c, i : i + 1, at]
                    total = term if total is None else total + term
                part[k, c, :, at] = total
                leave = jnp.sum(carry_col[k] * rhs_ref[c, :, at], axis=0, keepdims=True)
                t, o = (z * 128) // width, (z * 128) % width
                msg[k, t, c : c + 1, o : o + 128] = leave
                msg[k, t, 3 + c : 4 + c, o : o + 128] = total[0:1]

        first = []
        for d in range(1, rsize):
            to = lax.rem(place + d, rsize)
            first.append(
                send(msg.at[k, to], got1.at[k, place], s1s.at[k, d - 1], s1r.at[k, d - 1], (gx, line0 + to))
            )
        pending.extend(first)
        got1[k, place] = msg[k, place]
        if k < SECTIONS - 1:
            plane_copies = send_planes(k + 1, part.at[k])
            gather_plane(part.at[k], 0)
        for copy in first:
            copy.wait_recv()
        tiles = [got1[k, t] for t in range(rsize)]
        coefs = [coefficients(x) for x in tiles]
        e = jnp.where(sub == 6, 1.0, 0.0)
        starts = []
        for t in range(rsize):
            starts.append(e)
            e = down(tiles[t], coefs[t][0], e)
        l = jnp.where(sub == 7, 1.0, 0.0)
        for t in reversed(range(rsize)):
            l = up(tiles[t], coefs[t][1], coefs[t][2], starts[t], l)
        whole = jnp.where(
            (sub < 3) | (sub == 6),
            e,
            jnp.where((sub == 7) & (col < width // 2), pltpu.roll(l, 1, 0), l),
        )
        own2[k] = whole
        got2[k, line] = whole
        second = []
        for d in range(1, rows_n):
            to = lax.rem(line + d, rows_n)
            second.append(
                send(own2.at[k], got2.at[k, line], s2s.at[k, d - 1], s2r.at[k, d - 1], (gx, to * rsize + place))
            )
        pending.extend(second)
        for copy in second:
            copy.wait_recv()
        maps = [got2[k, q] for q in range(rows_n)]
        mcoefs = [coefficients(x) for x in maps]
        e = jnp.zeros((8, width), F32)
        e_row = jnp.zeros((8, width), F32)
        starts = []
        for q in range(rows_n):
            starts.append(e)
            e_row = jnp.where(line == q, e, e_row)
            e = down(maps[q], mcoefs[q][0], e)
        l = jnp.zeros((8, width), F32)
        l_row = jnp.zeros((8, width), F32)
        for q in reversed(range(rows_n)):
            l_row = jnp.where(line == q, l, l_row)
            l = up(maps[q], mcoefs[q][1], mcoefs[q][2], starts[q], l)
        e = jnp.where(sub < 3, e_row, 0.0)
        starts = []
        for t in range(rsize):
            starts.append(e)
            e = down(tiles[t], coefs[t][0], e)
        l = l_row
        for t in reversed(range(rsize)):
            ans[k, t] = jnp.where(sub < 3, starts[t], jnp.where(sub < 6, l, 0.0))
            l = up(tiles[t], coefs[t][1], coefs[t][2], starts[t], l)
        third = []
        for d in range(rsize):
            to = lax.rem(place + d, rsize)
            mate = line0 + to
            if d > 0:
                third.append(
                    send(ans.at[k, to], el.at[k, 0, place], s3s.at[k, 0, d], s3r.at[k, 0, d], (gx, mate))
                )
            if k < SECTIONS - 1:
                third.append(
                    send(ans.at[k, to], el.at[k, 1, place], s3s.at[k, 1, d], s3r.at[k, 1, d], (east, mate))
                )
                third.append(
                    send(ans.at[k, to], el.at[k, 2, place], s3s.at[k, 2, d], s3r.at[k, 2, d], (west, mate))
                )
        pending.extend(third)
        el[k, 0, place] = ans[k, place]
        if k < SECTIONS - 1:
            for copy in plane_copies:
                copy.wait_recv()
            gather_plane(planes.at[k + 1, 1], 1)
        else:
            for copy in trips:
                copy.wait_recv()
            part_out[:, 0:RESIDENT] = moved[0:3, 0:RESIDENT]
            part_out[:, RESIDENT : RESIDENT + CAP] = mig[0, 0:3, :]
            part_out[:, RESIDENT + CAP : RESIDENT + 2 * CAP] = mig[1, 0:3, :] * above_edge
            part_out[:, RESIDENT + 2 * CAP : RESIDENT + 3 * CAP] = mig[2, 0:3, :] * below_edge
        for copy in third:
            copy.wait_recv()

    rows = plane_rows(SECTIONS - 1, 0)
    k = SECTIONS - 1
    for c in range(comps):
        field_out[c] = part[k, c] + alpha[k] * rows[c : c + 1] + beta[k] * rows[3 + c : 4 + c]
    for copy in pending:
        copy.wait_send()


def on_device(
    velocity, y_metric, forward_rate, backward_rate, pivot_inv,
    particle_vel, particle_cell, particle_offset, inverse_tau, outgoing_count,
):
    comps, _, cy, cz = velocity.shape
    slots = particle_vel.shape[1]
    nx, lanes = lax.axis_size("gx"), lax.axis_size("gy")
    rsize = row_size(lanes)
    rows_n = lanes // rsize
    width = cz // rsize
    vmem, smem = pltpu.VMEM, pl.BlockSpec(memory_space=pltpu.SMEM)
    whole = pl.BlockSpec(memory_space=pltpu.VMEM)
    dma = pltpu.SemaphoreType.DMA
    scratch = [
        vmem((cz, slots), BF16),
        vmem((2, 2 * comps * cy, cz), BF16),
        vmem((2, 32, cz), BF16),
        vmem((2 * comps * cy, slots), BF16),
        vmem((comps * cy, cz), F32),
        vmem((8, slots), F32),
        vmem((cy, slots), F32),
        vmem((cy, slots), F32),
        vmem((SECTIONS, 8, slots), F32),
        vmem((8, slots), F32),
        vmem((8, slots), F32),
        vmem((1, slots), F32),
        vmem((8, slots), F32),
        vmem((SECTIONS, cy, cy, 128), F32),
        vmem((SECTIONS, cy, 128), F32),
        vmem((SECTIONS, cy, cz), F32),
        vmem((SECTIONS, cy, cz), F32),
        vmem((cy, cz), F32),
        vmem((cy, 128), F32),
        vmem((SECTIONS, comps, cy, cz), F32),
        vmem((SECTIONS, 2, comps, cy, cz), F32),
        vmem((comps, cy, cz), F32),
        vmem((comps, cy, cz), F32),
        vmem((8, cz), F32),
        vmem((3, 8, cz), F32),
        vmem((SECTIONS, rsize, 8, width), F32),
        vmem((SECTIONS, rsize, 8, width), F32),
        vmem((SECTIONS, rows_n, 8, width), F32),
        vmem((SECTIONS, 8, width), F32),
        vmem((SECTIONS, rsize, 8, width), F32),
        vmem((SECTIONS, 3, rsize, 8, width), F32),
        vmem((3, 8, CAP), F32),
        dma((SECTIONS, rsize - 1)), dma((SECTIONS, rsize - 1)),
        dma((SECTIONS, rows_n - 1)), dma((SECTIONS, rows_n - 1)),
        dma((SECTIONS, 3, rsize)), dma((SECTIONS, 3, rsize)),
        dma((SECTIONS, 2)), dma((SECTIONS, 2)),
        dma((3,)), dma((3,)), dma((3,)), dma((3,)),
    ]
    field, moved = pl.pallas_call(
        functools.partial(kernel, (nx, lanes, rsize)),
        out_shape=(
            jax.ShapeDtypeStruct((comps, cy, cz), F32),
            jax.ShapeDtypeStruct((comps, slots), F32),
        ),
        in_specs=[whole, smem, smem, smem, smem, whole, whole, whole, whole, smem],
        out_specs=(whole, whole),
        scratch_shapes=scratch,
        compiler_params=pltpu.CompilerParams(
            collective_id=0, has_side_effects=True, vmem_limit_bytes=48 * 1024 * 1024
        ),
        name="channel_sections",
    )(
        velocity.reshape(comps, cy, cz),
        y_metric,
        forward_rate,
        backward_rate,
        pivot_inv,
        particle_vel,
        particle_cell.reshape(1, slots),
        particle_offset,
        inverse_tau.reshape(1, slots),
        outgoing_count.reshape(3),
    )
    return field.reshape(velocity.shape), moved


def solution(mesh):
    return jax.shard_map(
        on_device,
        mesh=mesh,
        in_specs=(
            P(None, "gx", "gy", None),
            P("gy"),
            P(None, "gy"),
            P(None, "gy"),
            P(None, "gy"),
            P(None, ("gx", "gy")),
            P(("gx", "gy")),
            P(None, ("gx", "gy")),
            P(("gx", "gy")),
            P("gx", "gy", None),
        ),
        out_specs=(P(None, "gx", "gy", None), P(None, ("gx", "gy"))),
        check_vma=False,
    )
```

time: 1180 us -> 84.3 us (0.07)
  local copies, waits for them, and re-layouts: 570 us -> 4.57 us
  blocking collectives: 331 us -> 0 us
  other arithmetic: 229 us -> 0 us
  Pallas kernels: 0 us -> 78.7 us
  starting transfers between devices: 23.7 us -> 0 us
  waiting for transfers between devices: 12.8 us -> 0 us
    gather x48 -> x0, local copies, waits for them, and re-layouts: 428 us -> none  [on_device(): flat_ext[:, lookup]]
    all_gather x6 -> x0, blocking collectives: 265 us -> none  [carried_in(): gathered = jax.tree.map(lambda a: lax.all_gather(a, axis), part)]
    mul x12 -> x0, other arithmetic: 85.5 us -> none  [the longest x6 78.5 us: on_device(): extended = extended_2(field, (('gx', 1), ('gy', 2)), 1, True) * keep_rows]
    pallas_call x0 -> x1, Pallas kernels: none -> 78.7 us  [on_device(): pl.pallas_call(functools.partial(kernel, (nx, lanes, rsize)), out_shape=(...]
    scatter-add x3 -> x0, other arithmetic: 70.7 us -> none  [on_device(): force = jnp.zeros((comps, cells_x * cells_y * cells_z), jnp.float32).at[:...]
    unnamed x1 -> x0, blocking collectives: 66 us -> none
    add x95 -> x0, other arithmetic: 62.3 us -> none  [the longest x93 62.1 us: chain(): return (later[0] * earlier[0], later[0] * earlier[1] + later[1])]
    dynamic_slice x93 -> x0, local copies, waits for them, and re-layouts: 54.4 us -> none  [one(): lax.dynamic_index_in_dim(a, source, 0, False)]
  transfers between devices with their start and end apart: 15 -> 0, of which waited for: 9 -> 0; matrix products, arithmetic and copies ran while one was open for 3% -> 0% of each run, Pallas kernels for 0% -> 0%
where the time goes in v1:
time: 84.3 us; the launch traced here: 84.1 us
  Pallas kernels  78.7 us (93%)
  local copies, waits for them, and re-layouts  4.57 us (5%)
    pallas_call x1, Pallas kernels, on_device(): pl.pallas_call(functools.partial(kernel, (nx, lanes, rsize)), out_shape=(...  78.7 us
    unnamed x18, local copies, waits for them, and re-layouts  3.08 us

profile of v1, /device:TPU:1, one launch (start us, length us, event | category | flops | bytes accessed | tf_op | source)
XLA Modules:
  0.0 84.1 jit_solution(4653267019616022632)
XLA Ops:
  0.6 0.0 copy-start.1
  0.6 0.7 reshape.20.cell
  1.4 0.0 copy-start.3
  1.4 0.0 copy-start.4
  1.4 0.0 copy-start.5
  1.4 0.0 copy-start.6
  1.4 0.0 copy-start.7
  1.4 0.7 reshape.21.tau
  2.2 0.0 copy-done.1
  2.2 0.0 copy-done.3
  2.2 0.0 copy-done.4
  2.2 0.0 copy-done.5
  2.2 0.0 copy-done.6
  2.3 0.0 copy-done.7
  2.3 0.0 copy-start
  2.3 0.9 %copy-done = f32[3,1,16,1024]{3,2,1,0:T(8,128)S(1)} copy-done((f32[3,1,16,1024]{3,2,1,0:T(8,128)S(1)}, f32[3,1,16,1024]{3,2,1,0:T(8,128)}, u32[]{:S(2)}) %copy-start) | copy-done | bytes 196632
  3.2 0.0 copy-start.2
  3.2 0.8 copy-done.2
  4.0 78.7 %channel_sections.1 = (f32[3,16,1024]{2,1,0:T(8,128)S(1)}, f32[3,3584]{1,0:T(4,128)S(1)}) custom-call(f32[3,16,1024]{2,1,0:T(8,128)S(1)} %bitcast.6, f32[16]{0:T(128)S(1)} %copy-done.6, f32[3,16]{1,0:T(4,128)S(1)} %copy-done.3, f32[3,16]{1,0:T(4,128)S(1)} %copy-done.4, f32[3,16]{1,0:T(4,128)S(1)} %copy-done.5, f32[3,3584]{1,0:T(4,128)S(1)} %copy-done.1, ...), custom_call_target="tpu_custom_call" | custom-call | tf_op jit(solution)/shard_map/channel_sections/pallas_call | solution.py:515
  82.8 0.7 copy.15
  83.4 0.6 copy.16
Async XLA Ops:
  0.6 1.6 %copy-start.1 = (f32[3,3584]{1,0:T(4,128)S(1)}, f32[3,3584]{1,0:T(4,128)}, u32[]{:S(2)}) copy-start(f32[3,3584]{1,0:T(4,128)} %pvel.1) | copy-start | bytes 129028
  1.4 0.8 copy-start.3
  1.4 0.8 copy-start.4
  1.4 0.8 copy-start.5
  1.4 0.8 copy-start.6
  1.4 0.8 copy-start.7
  2.3 0.9 %copy-start = (f32[3,1,16,1024]{3,2,1,0:T(8,128)S(1)}, f32[3,1,16,1024]{3,2,1,0:T(8,128)}, u32[]{:S(2)}) copy-start(f32[3,1,16,1024]{3,2,1,0:T(8,128)} %param.10) | copy-start | bytes 589828
  3.2 0.8 copy-start.2

commit v2 on v1

--- a/solution.py
+++ b/solution.py
@@ -47,6 +47,7 @@
     chunk = min(CHUNK, slots)
     steps = slots // chunk
     last = cy - 1
+    rows6 = 2 * comps * cy
     gx = lax.axis_index("gx")
     gy = lax.axis_index("gy")
     place = lax.rem(gy, rsize)
@@ -189,19 +190,18 @@
         for c in range(comps):
             x = source[c]
             high, low = halves(x)
-            table[0, c * cy : (c + 1) * cy, :] = high
-            table[1, c * cy : (c + 1) * cy, :] = low
+            table[c * cy : (c + 1) * cy, :] = high
+            table[rows6 + c * cy : rows6 + (c + 1) * cy, :] = low
             high, low = halves(pltpu.roll(x, cz - 1, 1))
             at = (comps + c) * cy
-            table[0, at : at + cy, :] = high
-            table[1, at : at + cy, :] = low
-
-        def one(i, _):
-            at = pl.ds(pl.multiple_of(i * chunk, chunk), chunk)
+            table[at : at + cy, :] = high
+            table[rows6 + at : rows6 + at + cy, :] = low
+
+        def one(i):
+            at = slice(i * chunk, (i + 1) * chunk)
             hot = onehot[:, at]
-            got = jnp.dot(table[0], hot, preferred_element_type=F32) + jnp.dot(
-                table[1], hot, preferred_element_type=F32
-            )
+            got = jnp.dot(table[...], hot, preferred_element_type=F32)
+            got = got[0:rows6] + got[rows6 : 2 * rows6]
             w0 = wts[2 * side : 2 * side + 1, at]
             w1 = wts[2 * side + 1 : 2 * side + 2, at]
             w = ywt[:, at]
@@ -215,9 +215,9 @@
                 fluid[0:3, at] = value
             else:
                 fluid[0:3, at] = fluid[0:3, at] + value
-            return 0
-
-        lax.fori_loop(0, steps, one, 0)
+
+        for i in range(steps):
+            one(i)
 
     sub = lax.broadcasted_iota(jnp.int32, (8, width), 0)
     col = lax.broadcasted_iota(jnp.int32, (8, width), 1)
@@ -265,18 +265,17 @@
             own, minus, plus = plane_rows(k - 1, 0), plane_rows(k - 1, 1), plane_rows(k - 1, 2)
         pair = jnp.concatenate([own, plus], axis=0)
         high, low = halves(pair)
-        el_table[0, 0:16, :] = high
-        el_table[1, 0:16, :] = low
+        el_table[0:16, :] = high
+        el_table[32:48, :] = low
         high, low = halves(pltpu.roll(pair, cz - 1, 1))
-        el_table[0, 16:32, :] = high
-        el_table[1, 16:32, :] = low
-
-        def push(i, _, k=k, step=step):
-            at = pl.ds(pl.multiple_of(i * chunk, chunk), chunk)
+        el_table[16:32, :] = high
+        el_table[48:64, :] = low
+
+        def push(i, k=k, step=step):
+            at = slice(i * chunk, (i + 1) * chunk)
             hot = onehot[:, at]
-            got = jnp.dot(el_table[0], hot, preferred_element_type=F32) + jnp.dot(
-                el_table[1], hot, preferred_element_type=F32
-            )
+            got = jnp.dot(el_table[...], hot, preferred_element_type=F32)
+            got = got[0:32] + got[32:64]
             mix = (
                 wts[0:1, at] * got[0:8]
                 + wts[2:3, at] * got[8:16]
@@ -294,9 +293,9 @@
                 head = one.astype(BF16).astype(F32)
                 scat[c * cy : (c + 1) * cy, at] = (mask * head).astype(BF16)
                 scat[(comps + c) * cy : (comps + c + 1) * cy, at] = (mask * (one - head)).astype(BF16)
-            return 0
-
-        lax.fori_loop(0, steps, push, 0)
+
+        for i in range(steps):
+            push(i)
 
         if k == SECTIONS - 1:
             moved[...] = speed[...] * live_ref[...]
@@ -307,16 +306,16 @@
             ]
             pending.extend(trips)
 
-        def gathered(n, _):
-            at = pl.ds(pl.multiple_of(n * zblock, zblock), zblock)
+        def gathered(n):
+            at = slice(n * zblock, (n + 1) * zblock)
             both = lax.dot_general(
                 scat[...], onehot[at, :], (((1,), (1,)), ((), ())), preferred_element_type=F32
             )
             half = comps * cy
             accum[:, at] = both[0:half] + both[half : 2 * half]
-            return 0
-
-        lax.fori_loop(0, cz // zblock, gathered, 0)
+
+        for n in range(cz // zblock):
+            gathered(n)
 
         def plane(source, c, rows):
             if k == 0:
@@ -475,8 +474,8 @@
     dma = pltpu.SemaphoreType.DMA
     scratch = [
         vmem((cz, slots), BF16),
-        vmem((2, 2 * comps * cy, cz), BF16),
-        vmem((2, 32, cz), BF16),
+        vmem((4 * comps * cy, cz), BF16),
+        vmem((64, cz), BF16),
         vmem((2 * comps * cy, slots), BF16),
         vmem((comps * cy, cz), F32),
         vmem((8, slots), F32),

time: 84.3 us -> 73.5 us (0.87)
  Pallas kernels: 78.7 us -> 67.9 us
    pallas_call x1, Pallas kernels: 78.7 us -> 67.9 us  [on_device(): pl.pallas_call(functools.partial(kernel, (nx, lanes, rsize)), out_shape=(...]
where the time goes in v2:
time: 73.5 us; the launch traced here: 73.3 us
  Pallas kernels  67.9 us (92%)
  local copies, waits for them, and re-layouts  4.57 us (6%)
  between operations  0.75 us (1%)
    pallas_call x1, Pallas kernels, on_device(): pl.pallas_call(functools.partial(kernel, (nx, lanes, rsize)), out_shape=(...  67.9 us
    unnamed x18, local copies, waits for them, and re-layouts  3.08 us

profile of v2, /device:TPU:1, one launch (start us, length us, event | category | flops | bytes accessed | tf_op | source)
XLA Modules:
  0.0 73.3 jit_solution(8686801248439569042)
XLA Ops:
  0.6 0.0 copy-start.1
  0.6 0.7 %reshape.20.cell = s32[1,3584]{1,0:T(1,128)S(1)} reshape(s32[3584]{0:T(1024)} %param.16) | data formatting | bytes 28672 | tf_op jit(solution)/shard_map/reshape | solution.py:534
  1.4 0.0 copy-start.3
  1.4 0.0 copy-start.4
  1.4 0.0 copy-start.5
  1.4 0.0 copy-start.6
  1.4 0.0 copy-start.7
  1.4 0.7 %reshape.21.tau = f32[1,3584]{1,0:T(1,128)S(1)} reshape(f32[3584]{0:T(1024)} %param.18) | data formatting | bytes 28672 | tf_op jit(solution)/shard_map/reshape | solution.py:536
  2.2 0.0 copy-done.1
  2.2 0.0 copy-done.3
  2.2 0.0 copy-done.4
  2.2 0.0 copy-done.5
  2.2 0.0 copy-done.6
  2.3 0.0 copy-done.7
  2.3 0.0 copy-start
  2.3 0.9 %copy-done = f32[3,1,16,1024]{3,2,1,0:T(8,128)S(1)} copy-done((f32[3,1,16,1024]{3,2,1,0:T(8,128)S(1)}, f32[3,1,16,1024]{3,2,1,0:T(8,128)}, u32[]{:S(2)}) %copy-start) | copy-done | bytes 196632
  3.2 0.0 copy-start.2
  3.2 0.8 %copy-done.2 = f32[3,3584]{1,0:T(4,128)S(1)} copy-done((f32[3,3584]{1,0:T(4,128)S(1)}, f32[3,3584]{1,0:T(4,128)}, u32[]{:S(2)}) %copy-start.2) | copy-done | bytes 43032
  4.0 67.9 %channel_sections.1 = (f32[3,16,1024]{2,1,0:T(8,128)S(1)}, f32[3,3584]{1,0:T(4,128)S(1)}) custom-call(f32[3,16,1024]{2,1,0:T(8,128)S(1)} %bitcast.6, f32[16]{0:T(128)S(1)} %copy-done.6, f32[3,16]{1,0:T(4,128)S(1)} %copy-done.3, f32[3,16]{1,0:T(4,128)S(1)} %copy-done.4, f32[3,16]{1,0:T(4,128)S(1)} %copy-done.5, f32[3,3584]{1,0:T(4,128)S(1)} %copy-done.1, ...), custom_call_target="tpu_custom_call" | custom-call | tf_op jit(solution)/shard_map/channel_sections/pallas_call | solution.py:514
  71.9 0.7 copy.15
  72.6 0.6 copy.16
Async XLA Ops:
  0.6 1.6 %copy-start.1 = (f32[3,3584]{1,0:T(4,128)S(1)}, f32[3,3584]{1,0:T(4,128)}, u32[]{:S(2)}) copy-start(f32[3,3584]{1,0:T(4,128)} %pvel.1) | copy-start | bytes 129028
  1.4 0.8 %copy-start.3 = (f32[3,16]{1,0:T(4,128)S(1)}, f32[3,16]{1,0:T(4,128)}, u32[]{:S(2)}) copy-start(f32[3,16]{1,0:T(4,128)} %fwd.1) | copy-start | bytes 580
  1.4 0.8 %copy-start.4 = (f32[3,16]{1,0:T(4,128)S(1)}, f32[3,16]{1,0:T(4,128)}, u32[]{:S(2)}) copy-start(f32[3,16]{1,0:T(4,128)} %bwd.1) | copy-start | bytes 580
  1.4 0.8 %copy-start.5 = (f32[3,16]{1,0:T(4,128)S(1)}, f32[3,16]{1,0:T(4,128)}, u32[]{:S(2)}) copy-start(f32[3,16]{1,0:T(4,128)} %piv.1) | copy-start | bytes 580
  1.4 0.8 %copy-start.6 = (f32[16]{0:T(128)S(1)}, f32[16]{0:T(128)}, u32[]{:S(2)}) copy-start(f32[16]{0:T(128)} %metric.1) | copy-start | bytes 196
  1.4 0.8 %copy-start.7 = (s32[1,1,3]{2,1,0:T(1,128)S(1)}, s32[1,1,3]{2,1,0:T(1,128)}, u32[]{:S(2)}) copy-start(s32[1,1,3]{2,1,0:T(1,128)} %param.19) | copy-start | bytes 40
  2.3 0.9 %copy-start = (f32[3,1,16,1024]{3,2,1,0:T(8,128)S(1)}, f32[3,1,16,1024]{3,2,1,0:T(8,128)}, u32[]{:S(2)}) copy-start(f32[3,1,16,1024]{3,2,1,0:T(8,128)} %param.10) | copy-start | bytes 589828
  3.2 0.8 %copy-start.2 = (f32[3,3584]{1,0:T(4,128)S(1)}, f32[3,3584]{1,0:T(4,128)}, u32[]{:S(2)}) copy-start(f32[3,3584]{1,0:T(4,128)} %offset.1) | copy-start | bytes 129028

commit v3 on v2

--- a/solution.py
+++ b/solution.py
@@ -32,8 +32,9 @@
 
 def kernel(
     dims,
-    vel, metric, fwd, bwd, piv, pvel, cell, offset, tau, count,
+    vel_in, metric, fwd, bwd, piv, pvel_in, cell_in, offset_in, tau_in, count,
     field_out, part_out,
+    vel, pvel, cell, offset, tau, inputs_sem,
     onehot, table, el_table, scat, accum, wts, ymask, ywt, ab, speed, fluid, live_ref, moved,
     solve_cols, carry_col, alpha, beta, ymet, unit_rows,
     part, planes, uref, rhs_ref, edge, edge_in, msg, got1, got2, own2, ans, el, mig,
@@ -41,9 +42,9 @@
 ):
     nx, lanes, rsize = dims
     rows_n = lanes // rsize
-    comps, cy, cz = vel.shape
+    comps, cy, cz = vel_in.shape
     width = cz // rsize
-    slots = pvel.shape[1]
+    slots = pvel_in.shape[1]
     chunk = min(CHUNK, slots)
     steps = slots // chunk
     last = cy - 1
@@ -66,20 +67,25 @@
         copy.start()
         return copy
 
+    loads = [
+        pltpu.make_async_copy(src, dst, inputs_sem.at[n])
+        for n, (src, dst) in enumerate(
+            ((vel_in, vel), (cell_in, cell), (offset_in, offset), (pvel_in, pvel), (tau_in, tau))
+        )
+    ]
+    for load in loads:
+        load.start()
     partners = []
     for d in range(1, rsize):
         partners.append((gx, line0 + lax.rem(place + d, rsize)))
     for d in range(1, rows_n):
         partners.append((gx, lax.rem(line + d, rows_n) * rsize + place))
-    for d in range(rsize):
-        mate = line0 + lax.rem(place + d, rsize)
-        partners.append((west, mate))
-        partners.append((east, mate))
-    partners += [(gx, south), (gx, north), (west, south), (east, north)]
+    partners += [(west, gy), (east, gy), (gx, south), (gx, north), (west, south), (east, north)]
     barrier = pltpu.get_barrier_semaphore()
     for to in partners:
         pl.semaphore_signal(barrier, inc=1, device_id=to, device_id_type=MESH)
 
+    loads[0].wait()
     for c in range(comps):
         edge[c : c + 1, :] = vel[c, last : last + 1, :]
         edge[3 + c : 4 + c, :] = vel[c, 0:1, :]
@@ -105,6 +111,8 @@
     ]
     pending.extend(edge_copies)
 
+    for load in loads[1:]:
+        load.wait()
     row16 = lax.broadcasted_iota(jnp.int32, (cy, chunk), 0)
     lane = lax.broadcasted_iota(jnp.int32, (1, chunk), 1)
     zblock = min(256, cz)
@@ -115,7 +123,7 @@
 
     def prepare(i, _):
         at = pl.ds(pl.multiple_of(i * chunk, chunk), chunk)
-        where = cell[:, at]
+        where = cell[at].reshape(1, chunk)
         zpos = lax.rem(where, cz)
         ypos = lax.rem(lax.div(where, cz), cy)
         for n in range(cz // zblock):
@@ -248,9 +256,9 @@
     gather_plane(vel, 0)
     for copy in edge_copies:
         copy.wait_recv()
-    for copy in plane_copies:
-        copy.wait_recv()
+    plane_copies[0].wait_recv()
     gather_plane(planes.at[0, 1], 1)
+    behind = []
 
     for k in range(SECTIONS):
         step = TIME_STEP * SECTION_WEIGHTS[k]
@@ -260,9 +268,8 @@
             lower = jnp.where(sub_full < 3, 1.0, 0.0) * below_edge
             own = edge_in[0] * lower + edge_in[1] * upper
             plus = edge_in[2] * upper
-            minus = None
         else:
-            own, minus, plus = plane_rows(k - 1, 0), plane_rows(k - 1, 1), plane_rows(k - 1, 2)
+            own, plus = plane_rows(k - 1, 0), plane_rows(k - 1, 2)
         pair = jnp.concatenate([own, plus], axis=0)
         high, low = halves(pair)
         el_table[0:16, :] = high
@@ -284,7 +291,7 @@
             ) * ab[k, :, at]
             flow = fluid[:, at] + mix + pltpu.roll(mix, 5, 0)
             now = speed[:, at]
-            drag = tau[:, at] * (flow - now)
+            drag = tau[at].reshape(1, chunk) * (flow - now)
             speed[:, at] = now + step * drag
             share = drag * (-COUPLING * live_ref[:, at])
             mask = ymask[:, at]
@@ -316,6 +323,11 @@
 
         for n in range(cz // zblock):
             gathered(n)
+
+        plane_copies[1].wait_recv()
+        for copy in behind:
+            copy.wait_recv()
+        minus = plane_rows(k - 1, 1) if k > 0 else None
 
         def plane(source, c, rows):
             if k == 0:
@@ -420,26 +432,18 @@
         for t in reversed(range(rsize)):
             ans[k, t] = jnp.where(sub < 3, starts[t], jnp.where(sub < 6, l, 0.0))
             l = up(tiles[t], coefs[t][1], coefs[t][2], starts[t], l)
-        third = []
-        for d in range(rsize):
-            to = lax.rem(place + d, rsize)
-            mate = line0 + to
-            if d > 0:
-                third.append(
-                    send(ans.at[k, to], el.at[k, 0, place], s3s.at[k, 0, d], s3r.at[k, 0, d], (gx, mate))
+        third = {slot: [] for slot in range(3)}
+        routes = [(0, gx), (2, west), (1, east)] if k < SECTIONS - 1 else [(0, gx)]
+        for slot, column in routes:
+            for d in range(1 if slot == 0 else 0, rsize):
+                to = lax.rem(place + d, rsize)
+                third[slot].append(
+                    send(ans.at[k, to], el.at[k, slot, place], s3s.at[k, slot, d], s3r.at[k, slot, d], (column, line0 + to))
                 )
-            if k < SECTIONS - 1:
-                third.append(
-                    send(ans.at[k, to], el.at[k, 1, place], s3s.at[k, 1, d], s3r.at[k, 1, d], (east, mate))
-                )
-                third.append(
-                    send(ans.at[k, to], el.at[k, 2, place], s3s.at[k, 2, d], s3r.at[k, 2, d], (west, mate))
-                )
-        pending.extend(third)
+        pending.extend(third[0] + third[1] + third[2])
         el[k, 0, place] = ans[k, place]
         if k < SECTIONS - 1:
-            for copy in plane_copies:
-                copy.wait_recv()
+            plane_copies[0].wait_recv()
             gather_plane(planes.at[k + 1, 1], 1)
         else:
             for copy in trips:
@@ -448,8 +452,9 @@
             part_out[:, RESIDENT : RESIDENT + CAP] = mig[0, 0:3, :]
             part_out[:, RESIDENT + CAP : RESIDENT + 2 * CAP] = mig[1, 0:3, :] * above_edge
             part_out[:, RESIDENT + 2 * CAP : RESIDENT + 3 * CAP] = mig[2, 0:3, :] * below_edge
-        for copy in third:
+        for copy in third[0] + third[2]:
             copy.wait_recv()
+        behind = third[1]
 
     rows = plane_rows(SECTIONS - 1, 0)
     k = SECTIONS - 1
@@ -472,7 +477,14 @@
     vmem, smem = pltpu.VMEM, pl.BlockSpec(memory_space=pltpu.SMEM)
     whole = pl.BlockSpec(memory_space=pltpu.VMEM)
     dma = pltpu.SemaphoreType.DMA
+    far = pl.BlockSpec(memory_space=pltpu.HBM)
+
+    def stay(x):
+        return pltpu.with_memory_space_constraint(x, pltpu.HBM)
+
     scratch = [
+        vmem((comps, cy, cz), F32), vmem((comps, slots), F32), vmem((slots,), jnp.int32),
+        vmem((3, slots), F32), vmem((slots,), F32), dma((5,)),
         vmem((cz, slots), BF16),
         vmem((4 * comps * cy, cz), BF16),
         vmem((64, cz), BF16),
@@ -517,7 +529,7 @@
             jax.ShapeDtypeStruct((comps, cy, cz), F32),
             jax.ShapeDtypeStruct((comps, slots), F32),
         ),
-        in_specs=[whole, smem, smem, smem, smem, whole, whole, whole, whole, smem],
+        in_specs=[far, smem, smem, smem, smem, far, far, far, far, smem],
         out_specs=(whole, whole),
         scratch_shapes=scratch,
         compiler_params=pltpu.CompilerParams(
@@ -525,16 +537,16 @@
         ),
         name="channel_sections",
     )(
-        velocity.reshape(comps, cy, cz),
-        y_metric,
-        forward_rate,
-        backward_rate,
-        pivot_inv,
-        particle_vel,
-        particle_cell.reshape(1, slots),
-        particle_offset,
-        inverse_tau.reshape(1, slots),
-        outgoing_count.reshape(3),
+        stay(velocity.reshape(comps, cy, cz)),
+        stay(y_metric),
+        stay(forward_rate),
+        stay(backward_rate),
+        stay(pivot_inv),
+        stay(particle_vel),
+        stay(particle_cell),
+        stay(particle_offset),
+        stay(inverse_tau),
+        stay(outgoing_count.reshape(3)),
     )
     return field.reshape(velocity.shape), moved
 

time: 73.5 us -> 68.4 us (0.931)
  local copies, waits for them, and re-layouts: 4.57 us -> 1.3 us
  Pallas kernels: 67.9 us -> 66.3 us
    unnamed x18 -> x2, local copies, waits for them, and re-layouts: 3.08 us -> 1.3 us
    pallas_call x1, Pallas kernels: 67.9 us -> 66.3 us  [on_device(): pl.pallas_call(functools.partial(kernel, (nx, lanes, rsize)), out_shape=(...]
    reshape x2 -> x0, local copies, waits for them, and re-layouts: 1.49 us -> none  [the longest x1 0.75 us: on_device(): inverse_tau.reshape(1, slots)]
where the time goes in v3:
time: 68.4 us; the launch traced here: 68.3 us
  Pallas kernels  66.3 us (97%)
  local copies, waits for them, and re-layouts  1.3 us (2%)
    pallas_call x1, Pallas kernels, on_device(): pl.pallas_call(functools.partial(kernel, (nx, lanes, rsize)), out_shape=(...  66.3 us

profile of v3, /device:TPU:1, one launch (start us, length us, event | category | flops | bytes accessed | tf_op | source)
XLA Modules:
  0.0 68.3 jit_solution(10219308990379415069)
XLA Ops:
  0.6 66.3 %channel_sections.1 = (f32[3,16,1024]{2,1,0:T(8,128)S(1)}, f32[3,3584]{1,0:T(4,128)S(1)}) custom-call(f32[3,16,1024]{2,1,0:T(8,128)} %bitcast.6, f32[16]{0:T(128)} %metric.1, f32[3,16]{1,0:T(4,128)} %fwd.1, f32[3,16]{1,0:T(4,128)} %bwd.1, f32[3,16]{1,0:T(4,128)} %piv.1, f32[3,3584]{1,0:T(4,128)} %pvel_in.1, s32[3584]{0:T(1024)} %cell_in.1, ...), custom_call_target="tpu_custom_call" | custom-call | tf_op jit(solution)/shard_map/channel_sections/pallas_call | solution.py:526
  67.0 0.7 copy.15
  67.6 0.6 copy.16

commit v4 on v3

--- a/solution.py
+++ b/solution.py
@@ -32,15 +32,16 @@
 
 def kernel(
     dims,
-    vel_in, metric, fwd, bwd, piv, pvel_in, cell_in, offset_in, tau_in, count,
+    vel_in, metric_in, fwd_in, bwd_in, piv_in, pvel_in, cell_in, offset_in, tau_in, count_in,
     field_out, part_out,
     vel, pvel, cell, offset, tau, inputs_sem,
-    onehot, table, el_table, scat, accum, wts, ymask, ywt, ab, speed, fluid, live_ref, moved,
+    sm_metric, sm_fwd, sm_bwd, sm_piv, sm_count, onehot, hot_rows, table, scat, accum, wts, ymask, ywt, ab, speed, fluid, live_ref, moved,
     solve_cols, carry_col, alpha, beta, ymet, unit_rows,
     part, planes, uref, rhs_ref, edge, edge_in, msg, got1, got2, own2, ans, el, mig,
     s1s, s1r, s2s, s2r, s3s, s3r, pls, plr, eds, edr, mgs, mgr,
 ):
     nx, lanes, rsize = dims
+    metric, fwd, bwd, piv, count = sm_metric, sm_fwd, sm_bwd, sm_piv, sm_count
     rows_n = lanes // rsize
     comps, cy, cz = vel_in.shape
     width = cz // rsize
@@ -70,11 +71,13 @@
     loads = [
         pltpu.make_async_copy(src, dst, inputs_sem.at[n])
         for n, (src, dst) in enumerate(
-            ((vel_in, vel), (cell_in, cell), (offset_in, offset), (pvel_in, pvel), (tau_in, tau))
+            (
+                (vel_in, vel), (piv_in, piv), (bwd_in, bwd),
+                (cell_in, cell), (offset_in, offset), (pvel_in, pvel), (tau_in, tau),
+                (fwd_in, fwd), (metric_in, metric), (count_in, count),
+            )
         )
     ]
-    for load in loads:
-        load.start()
     partners = []
     for d in range(1, rsize):
         partners.append((gx, line0 + lax.rem(place + d, rsize)))
@@ -85,7 +88,10 @@
     for to in partners:
         pl.semaphore_signal(barrier, inc=1, device_id=to, device_id_type=MESH)
 
-    loads[0].wait()
+    for load in loads:
+        load.start()
+    for load in loads[:3]:
+        load.wait()
     for c in range(comps):
         edge[c : c + 1, :] = vel[c, last : last + 1, :]
         edge[3 + c : 4 + c, :] = vel[c, 0:1, :]
@@ -111,7 +117,7 @@
     ]
     pending.extend(edge_copies)
 
-    for load in loads[1:]:
+    for load in loads[3:]:
         load.wait()
     row16 = lax.broadcasted_iota(jnp.int32, (cy, chunk), 0)
     lane = lax.broadcasted_iota(jnp.int32, (1, chunk), 1)
@@ -194,7 +200,7 @@
 
     lax.fori_loop(0, steps, responses, 0)
 
-    def gather_plane(source, side):
+    def fill_table(source):
         for c in range(comps):
             x = source[c]
             high, low = halves(x)
@@ -205,27 +211,28 @@
             table[at : at + cy, :] = high
             table[rows6 + at : rows6 + at + cy, :] = low
 
-        def one(i):
+    def interpolate(got, side, at):
+        got = got[0:rows6] + got[rows6 : 2 * rows6]
+        w0 = wts[2 * side : 2 * side + 1, at]
+        w1 = wts[2 * side + 1 : 2 * side + 2, at]
+        w = ywt[:, at]
+        rows = []
+        for c in range(comps):
+            near = got[c * cy : (c + 1) * cy]
+            far = got[(comps + c) * cy : (comps + c + 1) * cy]
+            rows.append(jnp.sum((w0 * near + w1 * far) * w, axis=0, keepdims=True))
+        value = jnp.concatenate(rows, axis=0)
+        if side == 0:
+            fluid[0:3, at] = value
+        else:
+            fluid[0:3, at] = fluid[0:3, at] + value
+
+    def gather_plane(source, side):
+        fill_table(source)
+        for i in range(steps):
             at = slice(i * chunk, (i + 1) * chunk)
-            hot = onehot[:, at]
-            got = jnp.dot(table[...], hot, preferred_element_type=F32)
-            got = got[0:rows6] + got[rows6 : 2 * rows6]
-            w0 = wts[2 * side : 2 * side + 1, at]
-            w1 = wts[2 * side + 1 : 2 * side + 2, at]
-            w = ywt[:, at]
-            rows = []
-            for c in range(comps):
-                near = got[c * cy : (c + 1) * cy]
-                far = got[(comps + c) * cy : (comps + c + 1) * cy]
-                rows.append(jnp.sum((w0 * near + w1 * far) * w, axis=0, keepdims=True))
-            value = jnp.concatenate(rows, axis=0)
-            if side == 0:
-                fluid[0:3, at] = value
-            else:
-                fluid[0:3, at] = fluid[0:3, at] + value
-
-        for i in range(steps):
-            one(i)
+            got = jnp.dot(table[0 : 2 * rows6, :], onehot[:, at], preferred_element_type=F32)
+            interpolate(got, side, at)
 
     sub = lax.broadcasted_iota(jnp.int32, (8, width), 0)
     col = lax.broadcasted_iota(jnp.int32, (8, width), 1)
@@ -254,10 +261,16 @@
     above_edge = jnp.where(gy < lanes - 1, 1.0, 0.0).astype(F32)
 
     gather_plane(vel, 0)
+    wide = lax.broadcasted_iota(jnp.int32, (128, cz), 1)
+    for n in range(slots // 128):
+        zpos = lax.rem(cell[n * 128 : (n + 1) * 128].reshape(1, 128), cz)
+        column = jnp.transpose(jnp.broadcast_to(zpos.astype(F32), (128, 128))).astype(jnp.int32)
+        spread = jnp.concatenate([column] * (cz // 128), axis=1)
+        hot_rows[n * 128 : (n + 1) * 128, :] = jnp.where(wide == spread, 1.0, 0.0).astype(BF16)
     for copy in edge_copies:
         copy.wait_recv()
     plane_copies[0].wait_recv()
-    gather_plane(planes.at[0, 1], 1)
+    fill_table(planes.at[0, 1])
     behind = []
 
     for k in range(SECTIONS):
@@ -272,16 +285,20 @@
             own, plus = plane_rows(k - 1, 0), plane_rows(k - 1, 2)
         pair = jnp.concatenate([own, plus], axis=0)
         high, low = halves(pair)
-        el_table[0:16, :] = high
-        el_table[32:48, :] = low
+        table[2 * rows6 + 0 : 2 * rows6 + 16, :] = high
+        table[2 * rows6 + 32 : 2 * rows6 + 48, :] = low
         high, low = halves(pltpu.roll(pair, cz - 1, 1))
-        el_table[16:32, :] = high
-        el_table[48:64, :] = low
+        table[2 * rows6 + 16 : 2 * rows6 + 32, :] = high
+        table[2 * rows6 + 48 : 2 * rows6 + 64, :] = low
 
         def push(i, k=k, step=step):
             at = slice(i * chunk, (i + 1) * chunk)
             hot = onehot[:, at]
-            got = jnp.dot(el_table[...], hot, preferred_element_type=F32)
+            base = 2 * rows6 if k else 0
+            got = jnp.dot(table[base:, :], hot, preferred_element_type=F32)
+            if k == 0:
+                interpolate(got, 1, at)
+                got = got[2 * rows6 :]
             got = got[0:32] + got[32:64]
             mix = (
                 wts[0:1, at] * got[0:8]
@@ -316,7 +333,7 @@
         def gathered(n):
             at = slice(n * zblock, (n + 1) * zblock)
             both = lax.dot_general(
-                scat[...], onehot[at, :], (((1,), (1,)), ((), ())), preferred_element_type=F32
+                scat[...], hot_rows[:, at], (((1,), (0,)), ((), ())), preferred_element_type=F32
             )
             half = comps * cy
             accum[:, at] = both[0:half] + both[half : 2 * half]
@@ -391,7 +408,9 @@
             starts.append(e)
             e = down(tiles[t], coefs[t][0], e)
         l = jnp.where(sub == 7, 1.0, 0.0)
+        ends = [None] * rsize
         for t in reversed(range(rsize)):
+            ends[t] = l
             l = up(tiles[t], coefs[t][1], coefs[t][2], starts[t], l)
         whole = jnp.where(
             (sub < 3) | (sub == 6),
@@ -407,6 +426,13 @@
                 send(own2.at[k], got2.at[k, line], s2s.at[k, d - 1], s2r.at[k, d - 1], (gx, to * rsize + place))
             )
         pending.extend(second)
+        middle = (sub >= 3) & (sub < 6)
+        forms = []
+        for t in range(rsize):
+            base = jnp.where(sub < 3, starts[t], jnp.where(middle, ends[t], 0.0))
+            of_e = jnp.where(sub < 3, starts[t][6:7], jnp.where(middle, ends[t][6:7], 0.0))
+            of_l = jnp.where(middle, ends[t][7:8], 0.0)
+            forms.append((base, of_e, of_l))
         for copy in second:
             copy.wait_recv()
         maps = [got2[k, q] for q in range(rows_n)]
@@ -423,15 +449,10 @@
         for q in reversed(range(rows_n)):
             l_row = jnp.where(line == q, l, l_row)
             l = up(maps[q], mcoefs[q][1], mcoefs[q][2], starts[q], l)
-        e = jnp.where(sub < 3, e_row, 0.0)
-        starts = []
+        e = jnp.where(sub < 3, e_row, pltpu.roll(e_row, 3, 0))
         for t in range(rsize):
-            starts.append(e)
-            e = down(tiles[t], coefs[t][0], e)
-        l = l_row
-        for t in reversed(range(rsize)):
-            ans[k, t] = jnp.where(sub < 3, starts[t], jnp.where(sub < 6, l, 0.0))
-            l = up(tiles[t], coefs[t][1], coefs[t][2], starts[t], l)
+            base, of_e, of_l = forms[t]
+            ans[k, t] = base + of_e * e + of_l * l_row
         third = {slot: [] for slot in range(3)}
         routes = [(0, gx), (2, west), (1, east)] if k < SECTIONS - 1 else [(0, gx)]
         for slot, column in routes:
@@ -474,7 +495,7 @@
     rsize = row_size(lanes)
     rows_n = lanes // rsize
     width = cz // rsize
-    vmem, smem = pltpu.VMEM, pl.BlockSpec(memory_space=pltpu.SMEM)
+    vmem, smem_of = pltpu.VMEM, pltpu.SMEM
     whole = pl.BlockSpec(memory_space=pltpu.VMEM)
     dma = pltpu.SemaphoreType.DMA
     far = pl.BlockSpec(memory_space=pltpu.HBM)
@@ -484,10 +505,12 @@
 
     scratch = [
         vmem((comps, cy, cz), F32), vmem((comps, slots), F32), vmem((slots,), jnp.int32),
-        vmem((3, slots), F32), vmem((slots,), F32), dma((5,)),
+        vmem((3, slots), F32), vmem((slots,), F32), dma((10,)),
+        smem_of((cy,), F32), smem_of((SECTIONS, cy), F32), smem_of((SECTIONS, cy), F32),
+        smem_of((SECTIONS, cy), F32), smem_of((3,), jnp.int32),
         vmem((cz, slots), BF16),
-        vmem((4 * comps * cy, cz), BF16),
-        vmem((64, cz), BF16),
+        vmem((slots, cz), BF16),
+        vmem((4 * comps * cy + 64, cz), BF16),
         vmem((2 * comps * cy, slots), BF16),
         vmem((comps * cy, cz), F32),
         vmem((8, slots), F32),
@@ -529,7 +552,7 @@
             jax.ShapeDtypeStruct((comps, cy, cz), F32),
             jax.ShapeDtypeStruct((comps, slots), F32),
         ),
-        in_specs=[far, smem, smem, smem, smem, far, far, far, far, smem],
+        in_specs=[far] * 10,
         out_specs=(whole, whole),
         scratch_shapes=scratch,
         compiler_params=pltpu.CompilerParams(

time: 68.4 us -> 63.7 us (0.931)
  Pallas kernels: 66.3 us -> 61.6 us
    pallas_call x1, Pallas kernels: 66.3 us -> 61.6 us  [on_device(): pl.pallas_call(functools.partial(kernel, (nx, lanes, rsize)), out_shape=(...]
where the time goes in v4:
time: 63.7 us; the launch traced here: 63.6 us
  Pallas kernels  61.6 us (97%)
  local copies, waits for them, and re-layouts  1.3 us (2%)
  between operations  0.64 us (1%)
    pallas_call x1, Pallas kernels, on_device(): pl.pallas_call(functools.partial(kernel, (nx, lanes, rsize)), out_shape=(...  61.6 us
    unnamed x2, local copies, waits for them, and re-layouts  1.3 us

profile of v4, /device:TPU:1, one launch (start us, length us, event | category | flops | bytes accessed | tf_op | source)
XLA Modules:
  0.0 63.6 jit_solution(12365491548891134693)
XLA Ops:
  0.6 61.6 %channel_sections.1 = (f32[3,16,1024]{2,1,0:T(8,128)S(1)}, f32[3,3584]{1,0:T(4,128)S(1)}) custom-call(f32[3,16,1024]{2,1,0:T(8,128)} %bitcast.6, f32[16]{0:T(128)} %metric_in.1, f32[3,16]{1,0:T(4,128)} %fwd_in.1, f32[3,16]{1,0:T(4,128)} %bwd_in.1, f32[3,16]{1,0:T(4,128)} %piv_in.1, f32[3,3584]{1,0:T(4,128)} %pvel_in.1, s32[3584]{0:T(1024)} %cell_in.1, ...), custom_call_target="tpu_custom_call" | custom-call | tf_op jit(solution)/shard_map/channel_sections/pallas_call | solution.py:549
  62.3 0.7 %copy.15 = f32[3,1,16,1024]{3,2,1,0:T(8,128)} copy(f32[3,1,16,1024]{3,2,1,0:T(8,128)S(1)} %bitcast.5) | data formatting | bytes 393216
  63.0 0.6 copy.16

commit v5 on v4

--- a/solution.py
+++ b/solution.py
@@ -106,10 +106,10 @@
     def send_planes(k, src):
         a = send(src, planes.at[k, 1], pls.at[k, 0], plr.at[k, 0], (west, gy))
         b = send(src, planes.at[k, 0], pls.at[k, 1], plr.at[k, 1], (east, gy))
-        pending.extend([a, b])
         return a, b
 
     plane_copies = send_planes(0, vel)
+    pending.extend(plane_copies)
     edge_copies = [
         send(edge, edge_in.at[0], eds.at[0], edr.at[0], (gx, north)),
         send(edge, edge_in.at[1], eds.at[1], edr.at[1], (gx, south)),
@@ -122,7 +122,7 @@
     row16 = lax.broadcasted_iota(jnp.int32, (cy, chunk), 0)
     lane = lax.broadcasted_iota(jnp.int32, (1, chunk), 1)
     zblock = min(256, cz)
-    zrow = lax.broadcasted_iota(jnp.int32, (zblock, chunk), 0)
+    zrow = lax.broadcasted_iota(jnp.int32, (zblock, chunk), 0).astype(F32).astype(BF16)
     c0, c1, c2 = count[0], count[1], count[2]
     speed[...] = jnp.zeros_like(speed)
     fluid[...] = jnp.zeros_like(fluid)
@@ -133,9 +133,10 @@
         zpos = lax.rem(where, cz)
         ypos = lax.rem(lax.div(where, cz), cy)
         for n in range(cz // zblock):
+            key = jnp.where(lax.div(zpos, zblock) == n, lax.rem(zpos, zblock), 2 * zblock)
             onehot[n * zblock : (n + 1) * zblock, at] = jnp.where(
-                zrow + n * zblock == zpos, 1.0, 0.0
-            ).astype(BF16)
+                zrow == key.astype(F32).astype(BF16), jnp.bfloat16(1.0), jnp.bfloat16(0.0)
+            )
         ox, oy, oz = offset[0:1, at], offset[1:2, at], offset[2:3, at]
         here = row16 == ypos
         above = row16 == ypos + 1
@@ -157,7 +158,8 @@
     lax.fori_loop(0, steps, prepare, 0)
 
     lane128 = lax.broadcasted_iota(jnp.int32, (1, 128), 1)
-    for k in range(SECTIONS):
+
+    def rates(k):
         g = jnp.zeros((1, 128), F32)
         gs = []
         for j in range(cy):
@@ -182,23 +184,23 @@
             msg[k, t, 6:7, :] = jnp.full((1, width), weight, F32)
             half = lax.broadcasted_iota(jnp.int32, (1, width), 1) < width // 2
             msg[k, t, 7:8, :] = jnp.where(half, alpha[k, 0:1, 0:width], shrink)
+
+    rates(0)
     for j in range(cy):
         ymet[j : j + 1, :] = jnp.full((1, cz), 0.5 * metric[j], F32)
 
-    def responses(i, _):
-        at = pl.ds(pl.multiple_of(i * chunk, chunk), chunk)
-        top = wts[4:5, at]
-        w = ywt[:, at]
-        zero = jnp.zeros((3, chunk), F32)
+    def responses(k):
         two = jnp.zeros((2, chunk), F32)
-        ab[0, :, at] = jnp.concatenate([zero, top, top, top, two], axis=0)
-        for k in range(1, SECTIONS):
-            a = jnp.sum(w * alpha[k - 1, :, 0:1], axis=0, keepdims=True)
-            b = jnp.sum(w * beta[k - 1, :, 0:1], axis=0, keepdims=True) + top
-            ab[k, :, at] = jnp.concatenate([a, a, a, b, b, b, two], axis=0)
-        return 0
-
-    lax.fori_loop(0, steps, responses, 0)
+        for i in range(steps):
+            at = slice(i * chunk, (i + 1) * chunk)
+            top = wts[4:5, at]
+            if k == 0:
+                a, b = jnp.zeros((1, chunk), F32), top
+            else:
+                w = ywt[:, at]
+                a = jnp.sum(w * alpha[k - 1, :, 0:1], axis=0, keepdims=True)
+                b = jnp.sum(w * beta[k - 1, :, 0:1], axis=0, keepdims=True) + top
+            ab[:, at] = jnp.concatenate([a, a, a, b, b, b, two], axis=0)
 
     def fill_table(source):
         for c in range(comps):
@@ -261,6 +263,7 @@
     above_edge = jnp.where(gy < lanes - 1, 1.0, 0.0).astype(F32)
 
     gather_plane(vel, 0)
+    responses(0)
     wide = lax.broadcasted_iota(jnp.int32, (128, cz), 1)
     for n in range(slots // 128):
         zpos = lax.rem(cell[n * 128 : (n + 1) * 128].reshape(1, 128), cz)
@@ -305,7 +308,7 @@
                 + wts[2:3, at] * got[8:16]
                 + wts[1:2, at] * got[16:24]
                 + wts[3:4, at] * got[24:32]
-            ) * ab[k, :, at]
+            ) * ab[:, at]
             flow = fluid[:, at] + mix + pltpu.roll(mix, 5, 0)
             now = speed[:, at]
             drag = tau[at].reshape(1, chunk) * (flow - now)
@@ -330,6 +333,11 @@
             ]
             pending.extend(trips)
 
+        plane_copies[1].wait_recv()
+        for copy in behind:
+            copy.wait_recv()
+        minus = plane_rows(k - 1, 1) if k > 0 else None
+
         def gathered(n):
             at = slice(n * zblock, (n + 1) * zblock)
             both = lax.dot_general(
@@ -340,11 +348,6 @@
 
         for n in range(cz // zblock):
             gathered(n)
-
-        plane_copies[1].wait_recv()
-        for copy in behind:
-            copy.wait_recv()
-        minus = plane_rows(k - 1, 1) if k > 0 else None
 
         def plane(source, c, rows):
             if k == 0:
@@ -387,6 +390,8 @@
                 msg[k, t, c : c + 1, o : o + 128] = leave
                 msg[k, t, 3 + c : 4 + c, o : o + 128] = total[0:1]
 
+        if k == SECTIONS - 1:
+            sent, pending = pending, []
         first = []
         for d in range(1, rsize):
             to = lax.rem(place + d, rsize)
@@ -397,6 +402,7 @@
         got1[k, place] = msg[k, place]
         if k < SECTIONS - 1:
             plane_copies = send_planes(k + 1, part.at[k])
+            pending.extend(plane_copies)
             gather_plane(part.at[k], 0)
         for copy in first:
             copy.wait_recv()
@@ -433,6 +439,12 @@
             of_e = jnp.where(sub < 3, starts[t][6:7], jnp.where(middle, ends[t][6:7], 0.0))
             of_l = jnp.where(middle, ends[t][7:8], 0.0)
             forms.append((base, of_e, of_l))
+        if k < SECTIONS - 1:
+            rates(k + 1)
+            responses(k + 1)
+        else:
+            while sent:
+                sent.pop().wait_send()
         for copy in second:
             copy.wait_recv()
         maps = [got2[k, q] for q in range(rows_n)]
@@ -485,6 +497,17 @@
         copy.wait_send()
 
 
+def finish(field, moved, field_out, moved_out, sems):
+    copies = [
+        pltpu.make_async_copy(field, field_out, sems.at[0]),
+        pltpu.make_async_copy(moved, moved_out, sems.at[1]),
+    ]
+    for copy in copies:
+        copy.start()
+    for copy in copies:
+        copy.wait()
+
+
 def on_device(
     velocity, y_metric, forward_rate, backward_rate, pivot_inv,
     particle_vel, particle_cell, particle_offset, inverse_tau, outgoing_count,
@@ -516,7 +539,7 @@
         vmem((8, slots), F32),
         vmem((cy, slots), F32),
         vmem((cy, slots), F32),
-        vmem((SECTIONS, 8, slots), F32),
+        vmem((8, slots), F32),
         vmem((8, slots), F32),
         vmem((8, slots), F32),
         vmem((1, slots), F32),
@@ -571,6 +594,18 @@
         stay(inverse_tau),
         stay(outgoing_count.reshape(3)),
     )
+    field, moved = pl.pallas_call(
+        finish,
+        out_shape=(
+            jax.ShapeDtypeStruct((comps, cy, cz), F32),
+            jax.ShapeDtypeStruct((comps, slots), F32),
+        ),
+        in_specs=[whole, whole],
+        out_specs=(far, far),
+        scratch_shapes=[dma((2,))],
+        compiler_params=pltpu.CompilerParams(vmem_limit_bytes=4 * 1024 * 1024),
+        name="write_out",
+    )(field, moved)
     return field.reshape(velocity.shape), moved
 
 

time: 63.7 us -> 63 us (0.989)
  local copies, waits for them, and re-layouts: 1.3 us -> 0 us
    unnamed x2 -> x0, local copies, waits for them, and re-layouts: 1.3 us -> none
    pallas_call x0 -> x1, Pallas kernels: none -> 0.71 us  [on_device(): pl.pallas_call(finish, out_shape=(jax.ShapeDtypeStruct((comps, cy, cz), F...]
where the time goes in v5:
time: 63 us; the launch traced here: 62.9 us
  Pallas kernels  62.1 us (99%)
  between operations  0.8 us (1%)
    pallas_call x1, Pallas kernels, on_device(): pl.pallas_call(functools.partial(kernel, (nx, lanes, rsize)), out_shape=(...  61.4 us

profile of v5, /device:TPU:1, one launch (start us, length us, event | category | flops | bytes accessed | tf_op | source)
XLA Modules:
  0.0 62.9 jit_solution(5935537773380186262)
XLA Ops:
  0.6 61.4 %channel_sections.1 = (f32[3,16,1024]{2,1,0:T(8,128)S(1)}, f32[3,3584]{1,0:T(4,128)S(1)}) custom-call(f32[3,16,1024]{2,1,0:T(8,128)} %bitcast.5, f32[16]{0:T(128)} %metric_in.1, f32[3,16]{1,0:T(4,128)} %fwd_in.1, f32[3,16]{1,0:T(4,128)} %bwd_in.1, f32[3,16]{1,0:T(4,128)} %piv_in.1, f32[3,3584]{1,0:T(4,128)} %pvel_in.1, s32[3584]{0:T(1024)} %cell_in.1, ...), custom_call_target="tpu_custom_call" | custom-call | tf_op jit(solution)/shard_map/channel_sections/pallas_call | solution.py:572
  62.0 0.7 %write_out.1 = (f32[3,16,1024]{2,1,0:T(8,128)}, f32[3,3584]{1,0:T(4,128)}) custom-call(f32[3,16,1024]{2,1,0:T(8,128)S(1)} %get-tuple-element.6.field, f32[3,3584]{1,0:T(4,128)S(1)} %get-tuple-element.7.moved), custom_call_target="tpu_custom_call" | custom-call | tf_op jit(solution)/shard_map/write_out/pallas_call | solution.py:597

commit v6 on v5

--- a/solution.py
+++ b/solution.py
@@ -30,14 +30,21 @@
     return high, (x - high.astype(F32)).astype(BF16)
 
 
+def thirds(x):
+    high = x.astype(BF16)
+    rest = x - high.astype(F32)
+    low = rest.astype(BF16)
+    return high, low, (rest - low.astype(F32)).astype(BF16)
+
+
 def kernel(
     dims,
     vel_in, metric_in, fwd_in, bwd_in, piv_in, pvel_in, cell_in, offset_in, tau_in, count_in,
     field_out, part_out,
     vel, pvel, cell, offset, tau, inputs_sem,
     sm_metric, sm_fwd, sm_bwd, sm_piv, sm_count, onehot, hot_rows, table, scat, accum, wts, ymask, ywt, ab, speed, fluid, live_ref, moved,
-    solve_cols, carry_col, alpha, beta, ymet, unit_rows,
-    part, planes, uref, rhs_ref, edge, edge_in, msg, got1, got2, own2, ans, el, mig,
+    solve_mat, stacked, alpha, beta, ymet, unit_rows,
+    part, planes, uref, edge, edge_in, msg, got1, got2, own2, ans, el, mig,
     s1s, s1r, s2s, s2r, s3s, s3r, pls, plr, eds, edr, mgs, mgr,
 ):
     nx, lanes, rsize = dims
@@ -126,6 +133,7 @@
     c0, c1, c2 = count[0], count[1], count[2]
     speed[...] = jnp.zeros_like(speed)
     fluid[...] = jnp.zeros_like(fluid)
+    stacked[...] = jnp.zeros_like(stacked)
 
     def prepare(i, _):
         at = pl.ds(pl.multiple_of(i * chunk, chunk), chunk)
@@ -170,13 +178,16 @@
             u = piv[k, j] * gs[j] + bwd[k, j] * u
             unit_rows[j : j + 1, :] = u
         block = unit_rows[...]
-        for i in range(cy):
-            solve_cols[k, i] = jnp.broadcast_to(block[:, i : i + 1], (cy, 128))
+        full = jnp.concatenate([block, gs[last], jnp.zeros((cy - 1, 128), F32)], axis=0)
+        pa, pb, pc = (x.astype(F32) for x in thirds(full))
+        total = pa
+        for n, x in enumerate((pa, pa, pb, pb, pc)):
+            total = total + pltpu.roll(x, (n + 1) * cy, 1)
+        solve_mat[k] = total.astype(BF16)
         alpha[k] = jnp.broadcast_to(block[:, 0:1] * fwd[k, 0], (cy, cz))
         weight = jnp.float32(1.0)
         shrink = jnp.float32(1.0)
         for j in reversed(range(cy)):
-            carry_col[k, j : j + 1, :] = jnp.full((1, 128), weight, F32)
             weight = weight * fwd[k, j]
             shrink = shrink * bwd[k, j]
             beta[k, j : j + 1, :] = jnp.full((1, cz), shrink, F32)
@@ -375,20 +386,17 @@
             lower_y = jnp.where(rowz == 0, under, pltpu.roll(u, 1, 0))
             slope_y = (upper_y - lower_y) * ymet[...]
             convection = -(uref[0] * slope_x + uref[1] * slope_y + uref[2] * slope_z)
-            rhs_ref[c] = u + step * (convection + accum[c * cy : (c + 1) * cy, :])
-
-        for c in range(comps):
-            for z in range(cz // 128):
-                at = slice(z * 128, (z + 1) * 128)
-                total = None
-                for i in range(cy):
-                    term = solve_cols[k, i] * rhs_ref[c, i : i + 1, at]
-                    total = term if total is None else total + term
-                part[k, c, :, at] = total
-                leave = jnp.sum(carry_col[k] * rhs_ref[c, :, at], axis=0, keepdims=True)
-                t, o = (z * 128) // width, (z * 128) % width
-                msg[k, t, c : c + 1, o : o + 128] = leave
-                msg[k, t, 3 + c : 4 + c, o : o + 128] = total[0:1]
+            rhs = u + step * (convection + accum[c * cy : (c + 1) * cy, :])
+
+            pa, pb, pc = thirds(rhs)
+            for n, x in enumerate((pa, pb, pc, pa, pb, pa)):
+                stacked[c, n * cy : (n + 1) * cy, :] = x
+            solved = jnp.dot(solve_mat[k], stacked[c], preferred_element_type=F32)
+            part[k, c] = solved[0:cy]
+            for t in range(rsize):
+                at = slice(t * width, (t + 1) * width)
+                msg[k, t, c : c + 1, :] = solved[cy : cy + 1, at]
+                msg[k, t, 3 + c : 4 + c, :] = solved[0:1, at]
 
         if k == SECTIONS - 1:
             sent, pending = pending, []
@@ -544,15 +552,14 @@
         vmem((8, slots), F32),
         vmem((1, slots), F32),
         vmem((8, slots), F32),
-        vmem((SECTIONS, cy, cy, 128), F32),
-        vmem((SECTIONS, cy, 128), F32),
+        vmem((SECTIONS, 2 * cy, 128), BF16),
+        vmem((comps, 128, cz), BF16),
         vmem((SECTIONS, cy, cz), F32),
         vmem((SECTIONS, cy, cz), F32),
         vmem((cy, cz), F32),
         vmem((cy, 128), F32),
         vmem((SECTIONS, comps, cy, cz), F32),
         vmem((SECTIONS, 2, comps, cy, cz), F32),
-        vmem((comps, cy, cz), F32),
         vmem((comps, cy, cz), F32),
         vmem((8, cz), F32),
         vmem((3, 8, cz), F32),

time: 63 us -> 63.1 us (level)
  no operation moved by 1% of the time
where the time goes in v6:
time: 63.1 us; the launch traced here: 63 us
  Pallas kernels  62.2 us (99%)
  between operations  0.8 us (1%)
    pallas_call x1, Pallas kernels, on_device(): pl.pallas_call(functools.partial(kernel, (nx, lanes, rsize)), out_shape=(...  61.5 us

profile of v6, /device:TPU:1, one launch (start us, length us, event | category | flops | bytes accessed | tf_op | source)
XLA Modules:
  0.0 63.0 jit_solution(7886184612371235874)
XLA Ops:
  0.6 61.5 %channel_sections.1 = (f32[3,16,1024]{2,1,0:T(8,128)S(1)}, f32[3,3584]{1,0:T(4,128)S(1)}) custom-call(f32[3,16,1024]{2,1,0:T(8,128)} %bitcast.5, f32[16]{0:T(128)} %metric_in.1, f32[3,16]{1,0:T(4,128)} %fwd_in.1, f32[3,16]{1,0:T(4,128)} %bwd_in.1, f32[3,16]{1,0:T(4,128)} %piv_in.1, f32[3,3584]{1,0:T(4,128)} %pvel_in.1, s32[3584]{0:T(1024)} %cell_in.1, ...), custom_call_target="tpu_custom_call" | custom-call | tf_op jit(solution)/shard_map/channel_sections/pallas_call | solution.py:579
  62.1 0.7 %write_out.1 = (f32[3,16,1024]{2,1,0:T(8,128)}, f32[3,3584]{1,0:T(4,128)}) custom-call(f32[3,16,1024]{2,1,0:T(8,128)S(1)} %get-tuple-element.6.field, f32[3,3584]{1,0:T(4,128)S(1)} %get-tuple-element.7.moved), custom_call_target="tpu_custom_call" | custom-call | tf_op jit(solution)/shard_map/write_out/pallas_call | solution.py:604
